TPU v7x, 32 devices: a whole 2x2x4 slice. The times are simulated.
32 devices in a mesh: seq: 4 (over x, core), wide: 8 (over z, y).
Axes of the slice: x: 2, y: 2, z: 4, core: 2. Of those that a mesh axis runs over, the one named last changes fastest.
Arguments:
- tokens: bfloat16 [8, 512, 1536], P('wide', 'seq'), may hold values from -6 to 6
- segments: int32 [8, 512], P('wide'), may hold values from 0 to 3, never falling along the last dimension, each value on 1 to 256 neighbouring positions
- w_query: float32 [1536, 1536], P(('seq', 'wide')), may hold values from -0.15625 to 0.15625
- w_key: float32 [1536, 1536], P(('seq', 'wide')), may hold values from -0.15625 to 0.15625
- w_value: float32 [1536, 1536], P(('seq', 'wide')), may hold values from -0.15625 to 0.15625
- w_out: float32 [1536, 1536], P(('seq', 'wide')), may hold values from -0.15625 to 0.15625
- gain_attn: float32 [1536], P(('seq', 'wide')), may hold values from 0.5 to 1.5
- gain_group: float32 [1536], P(('seq', 'wide')), may hold values from 0.5 to 1.5
- gain_ffn: float32 [1536], P(('seq', 'wide')), may hold values from 0.5 to 1.5
- conv_kernel: float32 [16, 6, 11], replicated, may hold values from -1.2 to 1.2
- head_mix: float32 [16, 2], replicated, may hold values from 0.2 to 1
- w_gate: float32 [1536, 4096], P('seq', 'wide'), may hold values from -0.15625 to 0.15625
- w_up: float32 [1536, 4096], P('seq', 'wide'), may hold values from -0.15625 to 0.15625
- w_down: float32 [4096, 1536], P('wide', 'seq'), may hold values from -0.09375 to 0.09375
- cotangent: bfloat16 [8, 512, 1536], P('wide', 'seq'), may hold values from -6 to 6
Outputs:
- output: bfloat16 [8, 512, 1536], P('wide', 'seq')
- grad_tokens: bfloat16 [8, 512, 1536], P('wide', 'seq')
- grad_w_query: float32 [1536, 1536], P(('seq', 'wide'))
- grad_w_key: float32 [1536, 1536], P(('seq', 'wide'))
- grad_w_value: float32 [1536, 1536], P(('seq', 'wide'))
- grad_w_out: float32 [1536, 1536], P(('seq', 'wide'))
- grad_gain_attn: float32 [1536], P(('seq', 'wide'))
- grad_gain_group: float32 [1536], P(('seq', 'wide'))
- grad_gain_ffn: float32 [1536], P(('seq', 'wide'))
- grad_conv_kernel: float32 [16, 6, 11], replicated
- grad_head_mix: float32 [16, 2], replicated
- grad_w_gate: float32 [1536, 4096], P('seq', 'wide')
- grad_w_up: float32 [1536, 4096], P('seq', 'wide')
- grad_w_down: float32 [4096, 1536], P('wide', 'seq')
Inputs may be any that keep to these rules, and one draw needn't show every extreme that they name: `segments`: along a pack the segment ids never fall; each of the 4 documents of a pack holds 1 to 256 positions and one holds exactly 256.
All inputs are finite; a program needn't handle non-finite values.
Results may differ from a plain program's by a relative error of at most 0.019.
The roundings to bfloat16 on the way count: a program that leaves them out, or rounds other values in their place, can miss the bound.
Values may be sent and summed in bfloat16 or wider, within the bound.
No kernel may reach another device: no remote copies, remote signals or barrier semaphores. Data moves between devices by JAX's collectives and lax.ppermute only.
A program may use at most 320 MiB of HBM per device.

v0:
```python
import jax
import jax.numpy as jnp
from jax import lax
from jax.sharding import PartitionSpec as P

HEADS = 16
HEAD_DIM = 96
CQ = 6
CK = 11
GROUP = 2


precise = lax.Precision.HIGHEST
epsilon = 1e-05


def passed_along(value, axis, by):
    devices = lax.axis_size(axis)
    pairs = [(i, i + by) for i in range(devices) if 0 <= i + by < devices]
    return lax.ppermute(value, axis, pairs)


def extended(block, sides, width):
    for axis, dim in sides:
        count = lax.axis_size(axis)
        forward = [(i, i + 1) for i in range(count - 1)]
        backward = [(target, source) for source, target in forward]
        low = lax.ppermute(
            lax.slice_in_dim(block, block.shape[dim] - width, None, axis=dim), axis, forward
        )
        high = lax.ppermute(lax.slice_in_dim(block, 0, width, axis=dim), axis, backward)
        block = jnp.concatenate([low, block, high], axis=dim)
    return block


def rms_scaled(values, gain_vec):
    return (
        values * lax.rsqrt(jnp.mean(values * values, axis=-1, keepdims=True) + epsilon) * gain_vec
    )


def group_scaled(values, gain_vec):
    center = values - jnp.mean(values, axis=-1, keepdims=True)
    spread = jnp.mean(center * center, axis=-1, keepdims=True)
    return center * lax.rsqrt(spread + epsilon) * gain_vec


def tile_masks(seg_query, pos_query, seg_key, pos_key, valid_flag):
    query_rim = CQ - 1
    key_rim = CK // 2
    allowed = (
        (seg_query[:, None] == seg_key[None, :])
        & (pos_key[None, :] <= pos_query[:, None])
        & valid_flag
    )
    row_count = seg_query.shape[0] - query_rim
    row_masks = jnp.stack(
        [
            (
                seg_query[query_rim - shift_q : query_rim - shift_q + row_count]
                == seg_query[query_rim:]
            ).astype(jnp.float32)
            for shift_q in range(CQ)
        ]
    )
    final_mask = allowed[query_rim:, key_rim : key_rim + row_count]
    return (allowed, row_masks, final_mask)


def convolve(scores, allowed, row_masks, kernel):
    query_rim = CQ - 1
    key_rim = CK // 2
    row_count = scores.shape[1] - query_rim
    col_count = scores.shape[2] - 2 * key_rim
    masked = jnp.where(allowed[None], scores, 0.0)
    summed = jnp.zeros((scores.shape[0], row_count, col_count), jnp.float32)
    for shift_q in range(CQ):
        inner_sum = jnp.zeros((scores.shape[0], row_count, col_count), jnp.float32)
        for shift_k in range(CK):
            piece_view = masked[
                :,
                query_rim - shift_q : query_rim - shift_q + row_count,
                2 * key_rim - shift_k : 2 * key_rim - shift_k + col_count,
            ]
            inner_sum = inner_sum + kernel[:, shift_q, shift_k][:, None, None] * piece_view
        summed = summed + row_masks[shift_q][None, :, None] * inner_sum
    return summed


def mix_heads(probs, head_mix):
    lead_dims = probs.shape[:-3]
    tail_dims = probs.shape[-2:]
    grouped = probs.reshape(lead_dims + (HEADS // GROUP, GROUP) + tail_dims)
    mixing = head_mix.reshape(HEADS // GROUP, GROUP, GROUP)
    summed = jnp.zeros(lead_dims + (HEADS // GROUP, GROUP) + tail_dims, jnp.float32)
    for source in range(GROUP):
        summed = summed + mixing[:, :, source][:, :, None, None] * jnp.expand_dims(
            grouped[..., :, source, :, :], -3
        )
    return summed.reshape(probs.shape)


def unmix_heads(grads, head_mix):
    lead_dims = grads.shape[:-3]
    tail_dims = grads.shape[-2:]
    grouped = grads.reshape(lead_dims + (HEADS // GROUP, GROUP) + tail_dims)
    mixing = head_mix.reshape(HEADS // GROUP, GROUP, GROUP)
    summed = jnp.zeros(lead_dims + (HEADS // GROUP, GROUP) + tail_dims, jnp.float32)
    for target in range(GROUP):
        summed = summed + mixing[:, target, :][:, :, None, None] * jnp.expand_dims(
            grouped[..., :, target, :, :], -3
        )
    return summed.reshape(grads.shape)


def contract(left_op, right_op, left_dim, right_dim):
    return lax.dot_general(
        left_op,
        right_op,
        (((left_dim,), (right_dim,)), ((), ())),
        preferred_element_type=jnp.float32,
    )


def gather_attention(w_query, w_key, w_value, w_out, gain_attn, gain_group, gain_ffn):
    return (
        lax.all_gather(w_query.astype(jnp.bfloat16), ("seq", "wide"), axis=0, tiled=True),
        lax.all_gather(w_key.astype(jnp.bfloat16), ("seq", "wide"), axis=0, tiled=True),
        lax.all_gather(w_value.astype(jnp.bfloat16), ("seq", "wide"), axis=0, tiled=True),
        lax.all_gather(w_out.astype(jnp.bfloat16), ("seq", "wide"), axis=0, tiled=True),
        lax.all_gather(gain_attn.astype(jnp.bfloat16), ("seq", "wide"), axis=0, tiled=True),
        lax.all_gather(gain_group.astype(jnp.bfloat16), ("seq", "wide"), axis=0, tiled=True),
        lax.all_gather(gain_ffn.astype(jnp.bfloat16), ("seq", "wide"), axis=0, tiled=True),
    )


def collect_packets(own, reach_len):
    stored = jnp.zeros((reach_len,) + own.shape, own.dtype).at[0].set(own)

    def advance(turn_index, state_pair):
        packet, stored_now = state_pair
        packet = passed_along(packet, "seq", 1)
        return (packet, lax.dynamic_update_index_in_dim(stored_now, packet, turn_index, 0))

    return lax.fori_loop(1, reach_len, advance, (own, stored))[1]


def tile_logits(query_ext, packet, seg_query, pos_query, seg_key_pad, other_shard, token_count):
    key_rim = CK // 2
    key_ext = packet[: token_count + 2 * key_rim].reshape(
        token_count + 2 * key_rim, HEADS, HEAD_DIM
    )
    scores = jnp.einsum(
        "qhe,khe->hqk", query_ext, key_ext, preferred_element_type=jnp.float32
    ) * HEAD_DIM ** (-0.5)
    key_start = other_shard * token_count
    seg_key = lax.dynamic_slice_in_dim(
        seg_key_pad, jnp.maximum(key_start, 0), token_count + 2 * key_rim
    )
    pos_key = key_start - key_rim + jnp.arange(token_count + 2 * key_rim, dtype=jnp.int32)
    allowed, row_masks, final_mask = tile_masks(
        seg_query, pos_query, seg_key, pos_key, other_shard >= 0
    )
    return (scores, allowed, row_masks, final_mask, key_ext)


def shards(
    tokens,
    segments,
    w_query,
    w_key,
    w_value,
    w_out,
    gain_attn,
    gain_group,
    gain_ffn,
    conv_kernel,
    head_mix,
    w_gate,
    w_up,
    w_down,
    cotangent,
):
    token_count = tokens.shape[1]
    query_rim = CQ - 1
    key_rim = CK // 2
    width_all = HEADS * HEAD_DIM
    scaling = HEAD_DIM ** (-0.5)
    seq_count = lax.axis_size("seq")
    longest_doc = min(1024, token_count * seq_count // 2)
    reach_len = min(seq_count - 1, (longest_doc - 1) // token_count + 1) + 1
    seq_index = lax.axis_index("seq")
    row_start = seq_index * token_count
    seg_row = segments[0]
    seg_query_pad = jnp.concatenate([jnp.full((query_rim,), -1, jnp.int32), seg_row])
    seg_key_pad = jnp.concatenate(
        [jnp.full((key_rim,), -2, jnp.int32), seg_row, jnp.full((key_rim,), -2, jnp.int32)]
    )
    seg_query = lax.dynamic_slice_in_dim(seg_query_pad, row_start, token_count + query_rim)
    pos_query = row_start - query_rim + jnp.arange(token_count + query_rim, dtype=jnp.int32)
    weights = gather_attention(w_query, w_key, w_value, w_out, gain_attn, gain_group, gain_ffn)
    query_mat, key_mat, value_mat, out_mat, gain_one, gain_mid, gain_two = weights
    inputs = tokens[0].astype(jnp.float32)
    gain_first = gain_one.astype(jnp.float32)
    normed = rms_scaled(inputs, gain_first).astype(jnp.bfloat16)
    queries = jnp.dot(normed, query_mat, preferred_element_type=jnp.float32).astype(jnp.bfloat16)
    keys_loc = jnp.dot(normed, key_mat, preferred_element_type=jnp.float32).astype(jnp.bfloat16)
    values_loc = jnp.dot(normed, value_mat, preferred_element_type=jnp.float32).astype(jnp.bfloat16)
    rimmed = extended(jnp.stack([queries, keys_loc]), (("seq", 1),), key_rim)
    query_ext = rimmed[0, : token_count + query_rim].reshape(
        token_count + query_rim, HEADS, HEAD_DIM
    )
    own = jnp.concatenate([rimmed[1], values_loc], axis=0)
    packets = collect_packets(own, reach_len)

    def all_logits(packet_stack):

        def logits_of(turn_index):
            packet = lax.dynamic_index_in_dim(packet_stack, turn_index, 0, keepdims=False)
            scores, allowed, row_masks, final_mask, key_ext = tile_logits(
                query_ext,
                packet,
                seg_query,
                pos_query,
                seg_key_pad,
                seq_index - turn_index,
                token_count,
            )
            return jnp.where(
                final_mask[None], convolve(scores, allowed, row_masks, conv_kernel), -jnp.inf
            )

        return lax.map(logits_of, jnp.arange(reach_len, dtype=jnp.int32))

    logits = all_logits(packets)
    peak_val = jnp.max(logits, axis=(0, 3))
    log_total = peak_val + jnp.log(
        jnp.sum(jnp.exp(logits - peak_val[None, :, :, None]), axis=(0, 3))
    )
    probs_all = jnp.exp(logits - log_total[None, :, :, None])
    mixed_b = mix_heads(probs_all, head_mix).astype(jnp.bfloat16)
    values_all = packets[:, token_count + 2 * key_rim :].reshape(
        reach_len, token_count, HEADS, HEAD_DIM
    )
    attended = jnp.einsum("rhtk,rkhe->the", mixed_b, values_all, preferred_element_type=jnp.float32)
    gain_middle = gain_mid.astype(jnp.float32).reshape(HEADS, HEAD_DIM)
    grouped = (
        group_scaled(attended, gain_middle).reshape(token_count, width_all).astype(jnp.bfloat16)
    )
    middle = inputs + jnp.dot(grouped, out_mat, preferred_element_type=jnp.float32)
    gain_second = gain_two.astype(jnp.float32)
    ffn_in = rms_scaled(middle, gain_second).astype(jnp.bfloat16)
    ffn_all = lax.all_gather(ffn_in, "wide", axis=0, tiled=True)
    gate_mat, up_mat, down_mat = (
        lax.all_gather(w_gate.astype(jnp.bfloat16), "seq", axis=0, tiled=True),
        lax.all_gather(w_up.astype(jnp.bfloat16), "seq", axis=0, tiled=True),
        lax.all_gather(w_down.astype(jnp.bfloat16), "seq", axis=1, tiled=True),
    )
    gate_val = jnp.dot(ffn_all, gate_mat, preferred_element_type=jnp.float32)
    up_val = jnp.dot(ffn_all, up_mat, preferred_element_type=jnp.float32)
    hidden = (jax.nn.silu(gate_val) * up_val).astype(jnp.bfloat16)
    ffn_out = lax.psum_scatter(
        jnp.dot(hidden, down_mat, preferred_element_type=jnp.float32).astype(jnp.bfloat16),
        "wide",
        scatter_dimension=0,
        tiled=True,
    ).astype(jnp.float32)
    output = (middle + ffn_out).astype(jnp.bfloat16)
    grad_out = cotangent[0]
    grad_all = lax.all_gather(grad_out, "wide", axis=0, tiled=True)
    grad_hidden = contract(grad_all, down_mat, 1, 1)
    grad_down = contract(hidden, grad_all, 0, 0)
    sig_gate = jax.nn.sigmoid(gate_val)
    grad_gate = (grad_hidden * up_val * sig_gate * (1.0 + gate_val * (1.0 - sig_gate))).astype(
        jnp.bfloat16
    )
    grad_up = (grad_hidden * gate_val * sig_gate).astype(jnp.bfloat16)
    grad_gate_w = contract(ffn_all, grad_gate, 0, 0)
    grad_up_w = contract(ffn_all, grad_up, 0, 0)
    grad_ffn_in = lax.psum_scatter(
        (contract(grad_gate, gate_mat, 1, 1) + contract(grad_up, up_mat, 1, 1)).astype(
            jnp.bfloat16
        ),
        "wide",
        scatter_dimension=0,
        tiled=True,
    ).astype(jnp.float32)
    ffn_grads = (
        lax.psum_scatter(
            grad_gate_w.astype(jnp.bfloat16), "seq", scatter_dimension=0, tiled=True
        ).astype(jnp.float32),
        lax.psum_scatter(
            grad_up_w.astype(jnp.bfloat16), "seq", scatter_dimension=0, tiled=True
        ).astype(jnp.float32),
        lax.psum_scatter(
            grad_down.astype(jnp.bfloat16), "seq", scatter_dimension=1, tiled=True
        ).astype(jnp.float32),
    )
    norm_two_back = jax.vjp(rms_scaled, middle, gain_second)[1]
    grad_mid_part, grad_gain_two = norm_two_back(grad_ffn_in)
    grad_middle = grad_out.astype(jnp.float32) + grad_mid_part
    grad_branch = grad_middle.astype(jnp.bfloat16)
    back_weights = gather_attention(w_query, w_key, w_value, w_out, gain_attn, gain_group, gain_ffn)
    query_back, key_back, value_back, out_back = (
        back_weights[0],
        back_weights[1],
        back_weights[2],
        back_weights[3],
    )
    grad_grouped = contract(grad_branch, out_back, 1, 1)
    grad_out_w = contract(grouped, grad_branch, 0, 0)
    group_back = jax.vjp(group_scaled, attended, gain_middle)[1]
    grad_attended, grad_gain_mid = group_back(grad_grouped.reshape(token_count, HEADS, HEAD_DIM))
    grad_att_b = grad_attended.astype(jnp.bfloat16)
    back_packets = collect_packets(own, reach_len)
    logits_again = all_logits(back_packets)
    probs_again = jnp.exp(logits_again - log_total[None, :, :, None])
    mixed_again = mix_heads(probs_again, head_mix).astype(jnp.bfloat16)
    values_back = back_packets[:, token_count + 2 * key_rim :].reshape(
        reach_len, token_count, HEADS, HEAD_DIM
    )
    grad_mixed = jnp.einsum(
        "the,rkhe->rhtk", grad_att_b, values_back, preferred_element_type=jnp.float32
    )
    grad_values = jnp.einsum(
        "rhtk,the->rkhe", mixed_again, grad_att_b, preferred_element_type=jnp.float32
    ).reshape(reach_len, token_count, width_all)
    probs_grouped = probs_again.reshape(reach_len, HEADS // GROUP, GROUP, token_count, token_count)
    mixed_grouped = grad_mixed.reshape(reach_len, HEADS // GROUP, GROUP, token_count, token_count)
    grad_mix = jnp.einsum(
        "rgdtk,rgctk->gcd", probs_grouped, mixed_grouped, precision=precise
    ).reshape(HEADS, GROUP)
    grad_probs = unmix_heads(grad_mixed, head_mix)
    delta_row = jnp.sum(probs_again * grad_probs, axis=(0, 3))
    grad_logits = probs_again * (grad_probs - delta_row[None, :, :, None])

    def tile_grads(turn_index):
        packet = lax.dynamic_index_in_dim(back_packets, turn_index, 0, keepdims=False)
        scores, allowed, row_masks, final_mask, key_ext = tile_logits(
            query_ext,
            packet,
            seg_query,
            pos_query,
            seg_key_pad,
            seq_index - turn_index,
            token_count,
        )
        conv_back = jax.vjp(
            lambda field, weights_k: convolve(field, allowed, row_masks, weights_k),
            scores,
            conv_kernel,
        )[1]
        grad_scores, grad_kernel = conv_back(
            lax.dynamic_index_in_dim(grad_logits, turn_index, 0, keepdims=False)
        )
        grad_scores_b = grad_scores.astype(jnp.bfloat16)
        grad_query_ext = (
            jnp.einsum("hqk,khe->qhe", grad_scores_b, key_ext, preferred_element_type=jnp.float32)
            * scaling
        )
        grad_key_ext = (
            jnp.einsum("hqk,qhe->khe", grad_scores_b, query_ext, preferred_element_type=jnp.float32)
            * scaling
        )
        cycle_term = jnp.concatenate(
            [
                grad_key_ext.reshape(token_count + 2 * key_rim, width_all),
                lax.dynamic_index_in_dim(grad_values, turn_index, 0, keepdims=False),
            ],
            axis=0,
        )
        return (cycle_term, grad_query_ext, grad_kernel)

    start_term, start_query, start_kernel = tile_grads(reach_len - 1)

    def descend(turn_index, state_all):
        cycle_acc, query_acc, kernel_acc = state_all
        cycle_term, query_part, kernel_part = tile_grads(reach_len - 1 - turn_index)
        moved_acc = passed_along(cycle_acc.astype(jnp.bfloat16), "seq", -1).astype(cycle_acc.dtype)
        return (moved_acc + cycle_term, query_acc + query_part, kernel_acc + kernel_part)

    cycle_acc, query_acc, kernel_acc = lax.fori_loop(
        1, reach_len, descend, (start_term, start_query, start_kernel)
    )
    query_flat = query_acc.reshape(token_count + query_rim, width_all)
    key_ext_grad = cycle_acc[: token_count + 2 * key_rim]
    grad_values_own = cycle_acc[token_count + 2 * key_rim :]
    edge_grads = jnp.stack(
        [
            jnp.concatenate([query_flat[:query_rim], jnp.zeros((key_rim, width_all), jnp.float32)]),
            jnp.concatenate([key_ext_grad[:key_rim], key_ext_grad[token_count + key_rim :]]),
        ]
    )
    rim_back = extended(edge_grads.astype(jnp.bfloat16), (("seq", 1),), key_rim).astype(
        edge_grads.dtype
    )
    grad_queries = (
        query_flat[query_rim:].at[token_count - key_rim :].add(rim_back[0, 3 * key_rim :])
    )
    grad_keys = (
        key_ext_grad[key_rim : key_rim + token_count]
        .at[:key_rim]
        .add(rim_back[1, :key_rim])
        .at[token_count - key_rim :]
        .add(rim_back[1, 3 * key_rim :])
    )
    grad_query_b = grad_queries.astype(jnp.bfloat16)
    grad_key_b = grad_keys.astype(jnp.bfloat16)
    grad_value_b = grad_values_own.astype(jnp.bfloat16)
    grad_query_w = contract(normed, grad_query_b, 0, 0)
    grad_key_w = contract(normed, grad_key_b, 0, 0)
    grad_value_w = contract(normed, grad_value_b, 0, 0)
    grad_normed = (
        contract(grad_query_b, query_back, 1, 1)
        + contract(grad_key_b, key_back, 1, 1)
        + contract(grad_value_b, value_back, 1, 1)
    )
    norm_one_back = jax.vjp(rms_scaled, inputs, gain_first)[1]
    grad_in_part, grad_gain_one = norm_one_back(grad_normed)
    grad_input = (grad_middle + grad_in_part).astype(jnp.bfloat16)
    attn_grads = (
        lax.psum_scatter(grad_query_w, ("seq", "wide"), scatter_dimension=0, tiled=True),
        lax.psum_scatter(grad_key_w, ("seq", "wide"), scatter_dimension=0, tiled=True),
        lax.psum_scatter(grad_value_w, ("seq", "wide"), scatter_dimension=0, tiled=True),
        lax.psum_scatter(grad_out_w, ("seq", "wide"), scatter_dimension=0, tiled=True),
        lax.psum_scatter(grad_gain_one, ("seq", "wide"), scatter_dimension=0, tiled=True),
        lax.psum_scatter(
            grad_gain_mid.reshape(width_all), ("seq", "wide"), scatter_dimension=0, tiled=True
        ),
        lax.psum_scatter(grad_gain_two, ("seq", "wide"), scatter_dimension=0, tiled=True),
    )
    small_sums = lax.psum((kernel_acc, grad_mix), ("seq", "wide"))
    return (
        output[None],
        grad_input[None],
        attn_grads[0],
        attn_grads[1],
        attn_grads[2],
        attn_grads[3],
        attn_grads[4],
        attn_grads[5],
        attn_grads[6],
        small_sums[0],
        small_sums[1],
        ffn_grads[0],
        ffn_grads[1],
        ffn_grads[2],
    )


def solution(mesh):
    return jax.shard_map(
        shards,
        mesh=mesh,
        in_specs=(
            P("wide", "seq", None),
            P("wide", None),
            P(("seq", "wide"), None),
            P(("seq", "wide"), None),
            P(("seq", "wide"), None),
            P(("seq", "wide"), None),
            P(("seq", "wide")),
            P(("seq", "wide")),
            P(("seq", "wide")),
            P(),
            P(),
            P("seq", "wide"),
            P("seq", "wide"),
            P("wide", "seq"),
            P("wide", "seq", None),
        ),
        out_specs=(
            P("wide", "seq", None),
            P("wide", "seq", None),
            P(("seq", "wide"), None),
            P(("seq", "wide"), None),
            P(("seq", "wide"), None),
            P(("seq", "wide"), None),
            P(("seq", "wide")),
            P(("seq", "wide")),
            P(("seq", "wide")),
            P(),
            P(),
            P("seq", "wide"),
            P("seq", "wide"),
            P("wide", "seq"),
        ),
        check_vma=False,
    )
```

profile of v0, /device:TPU:0, one launch (start us, length us, event | category | flops | bytes accessed | tf_op | source)
XLA Modules:
  0.0 1519.8 jit_solution(18388940219064234004)
XLA Ops:
  16.2 42.2 %all-reduce.274 = (bf16[1536]{0:T(1024)(128)(2,1)S(1)}, bf16[1536]{0:T(1024)(128)(2,1)S(1)}, bf16[1536]{0:T(1024)(128)(2,1)S(1)}) all-reduce(bf16[1536]{0:T(1024)(128)(2,1)S(1)} %dynamic-update-slice.13, bf16[1536]{0:T(1024)(128)(2,1)S(1)} %dynamic-update-slice.14, ...), channel_id=1, replica_groups=mesh['seq'=4,'wide'=8] {'seq','wide'}, use_global_device_ids=true, to_apply=%add.267 | all-reduce | flops 4608 | bytes 18432
  60.1 18.1 %all-gather.13.cloned.1.call-done = bf16[1536,1536]{1,0:T(8,128)(2,1)} async-done(((bf16[48,1536]{1,0:T(8,128)(2,1)}), bf16[1536,1536]{1,0:T(8,128)(2,1)}) %all-gather.13.cloned.1.call-update) | async-done | bytes 4718608 | tf_op jit(solution)/shard_map/all_gather | solution.py:128
  81.4 62.9 %all-gather.11.cloned.1.call-done = bf16[1536,1536]{1,0:T(8,128)(2,1)} async-done(((bf16[48,1536]{1,0:T(8,128)(2,1)}), bf16[1536,1536]{1,0:T(8,128)(2,1)}) %all-gather.11.cloned.1.call-update) | async-done | bytes 4718608 | tf_op jit(solution)/shard_map/all_gather | solution.py:127
  151.1 59.2 %all-gather.15.cloned.1.call-done = bf16[1536,1536]{1,0:T(8,128)(2,1)} async-done(((bf16[48,1536]{1,0:T(8,128)(2,1)}), bf16[1536,1536]{1,0:T(8,128)(2,1)}) %all-gather.15.cloned.1.call-update) | async-done | bytes 4718608 | tf_op jit(solution)/shard_map/all_gather | solution.py:129
  216.9 19.9 %while.63 = (s32[]{:T(128)}, bf16[266,1536]{1,0:T(8,128)(2,1)S(1)}, bf16[3,266,1536]{2,1,0:T(8,128)(2,1)}, s32[]{:T(128)}, s32[]{:T(128)}, /*index=5*/s32[]{:T(128)}) while((s32[]{:T(128)}, bf16[266,1536]{1,0:T(8,128)(2,1)S(1)}, bf16[3,266,1536]{2,1,0:T(8,128)(2,1)}, s32[]{:T(128)}, s32[]{:T(128)}, /*index=5*/s32[]{:T(128)}) %tuple.681), condition=%wide.region_2.3_spmd, body=%wide.region_1.0_spmd.sunk | while | flops 5 | bytes 6555795 | solution.py:145
  222.1 11.8 collective-permute-start
  236.8 76.3 %while.64 = (s32[]{:T(128)}, f32[3,16,128,128]{3,2,1,0:T(8,128)}, s32[133]{0:T(256)S(1)}, s32[3]{0:T(128)S(1)}, s32[]{:T(128)}, /*index=5*/s32[522]{0:T(1024)S(1...) while((s32[]{:T(128)}, f32[3,16,128,128]{3,2,1,0:T(8,128)}, ...), condition=%wide.region_4.5_spmd.clone, body=%wide.region_3.4_spmd.clone.sunk | while | flops 92958880 | bytes 74066456 | solution.py:233
  242.5 19.8 %fusion.360 = f32[3,16,128,128]{3,2,1,0:T(8,128)} fusion(f32[3,16,128,128]{3,2,1,0:T(8,128)} %get-tuple-element.2229, s32[]{:T(128)S(6)} %copy.187, f32[16,133,138]{2,1,0:T(8,128)S(1)} %bitcast_select_fusion.4, f32[16]{0:T(128)S(1)} %get-tuple-element.1908, f32[16]{0:T(128)S(1)} %get-tuple-element.1909, f32[16]{0:T(128)S(1)} %get-tuple-element.1910, ...), kind=kLoop, calls=%fused_computation.10.clone.1 | loop fusion | flops 35913728 | bytes 70277760 | tf_op jit(solution)/shard_map/while/body/jit(dynamic_update_index_in_dim)/dynamic_update_slice | solution.py:233
  268.0 19.8 %fusion.360 = f32[3,16,128,128]{3,2,1,0:T(8,128)} fusion(f32[3,16,128,128]{3,2,1,0:T(8,128)} %get-tuple-element.2229, s32[]{:T(128)S(6)} %copy.187, f32[16,133,138]{2,1,0:T(8,128)S(1)} %bitcast_select_fusion.4, f32[16]{0:T(128)S(1)} %get-tuple-element.1908, f32[16]{0:T(128)S(1)} %get-tuple-element.1909, f32[16]{0:T(128)S(1)} %get-tuple-element.1910, ...), kind=kLoop, calls=%fused_computation.10.clone.1 | loop fusion | flops 35913728 | bytes 70277760 | tf_op jit(solution)/shard_map/while/body/jit(dynamic_update_index_in_dim)/dynamic_update_slice | solution.py:233
  293.4 19.8 %fusion.360 = f32[3,16,128,128]{3,2,1,0:T(8,128)} fusion(f32[3,16,128,128]{3,2,1,0:T(8,128)} %get-tuple-element.2229, s32[]{:T(128)S(6)} %copy.187, f32[16,133,138]{2,1,0:T(8,128)S(1)} %bitcast_select_fusion.4, f32[16]{0:T(128)S(1)} %get-tuple-element.1908, f32[16]{0:T(128)S(1)} %get-tuple-element.1909, f32[16]{0:T(128)S(1)} %get-tuple-element.1910, ...), kind=kLoop, calls=%fused_computation.10.clone.1 | loop fusion | flops 35913728 | bytes 70277760 | tf_op jit(solution)/shard_map/while/body/jit(dynamic_update_index_in_dim)/dynamic_update_slice | solution.py:233
  340.1 71.7 %all-gather.19.cloned.1.call-done = bf16[1024,1536]{1,0:T(8,128)(2,1)} async-done(((bf16[128,1536]{1,0:T(8,128)(2,1)}), bf16[1024,1536]{1,0:T(8,128)(2,1)}) %all-gather.19.cloned.1.call-update) | async-done | bytes 3145744 | tf_op jit(solution)/shard_map/all_gather | solution.py:253
  417.3 15.0 all-gather.21.cloned.1.call-done
  437.7 15.8 %all-gather.25.cloned.1.call-done = bf16[512,1536]{1,0:T(8,128)(2,1)} async-done(((bf16[512,384]{1,0:T(8,128)(2,1)}), bf16[512,1536]{1,0:T(8,128)(2,1)}) %all-gather.25.cloned.1.call-update) | async-done | bytes 1572880 | tf_op jit(solution)/shard_map/all_gather | solution.py:257
  453.5 62.7 %all-gather.27.cloned.1.call-done = bf16[1,1024,1536]{2,1,0:T(8,128)(2,1)} async-done(((bf16[1,128,1536]{2,1,0:T(8,128)(2,1)}), bf16[1,1024,1536]{2,1,0:T(8,128)(2,1)}) %all-gather.27.cloned.1.call-update) | async-done | bytes 3145744 | tf_op jit(solution)/shard_map/all_gather | solution.py:270
  559.0 43.2 %reduce-scatter.14.cloned.1.call-done = bf16[128,1536]{1,0:T(8,128)(2,1)} async-done(((bf16[1024,1536]{1,0:T(8,128)(2,1)}), bf16[128,1536]{1,0:T(8,128)(2,1)}) %reduce-scatter.14.cloned.1.call-update) | async-done | bytes 393232 | tf_op jit(solution)/shard_map/reduce_scatter | solution.py:280
  605.5 73.9 %reduce-scatter.12.cloned.1.call-done = bf16[128,1536]{1,0:T(8,128)(2,1)} async-done(((bf16[1024,1536]{1,0:T(8,128)(2,1)}), bf16[128,1536]{1,0:T(8,128)(2,1)}) %reduce-scatter.12.cloned.1.call-update) | async-done | bytes 393232 | tf_op jit(solution)/shard_map/reduce_scatter | solution.py:262
  767.7 42.2 %select_convert_fusion.1 = bf16[16,133,138]{2,1,0:T(8,128)(2,1)S(1)} fusion(f32[16,128,128]{2,1,0:T(8,128)} %get-tuple-element.1343, f32[16,128,128]{2,1,0:T(8,128)} %get-tuple-element.1342, f32[16,128,128]{2,1,0:T(8,128)} %get-tuple-element.1341, f32[16,128,128]{2,1,0:T(8,128)} %get-tuple-element.1340, f32[16,128,128]{2,1,0:T(8,128)} %get-tuple-element.1339, ...), kind=kLoop, calls=%fused_computation.529 | loop fusion | flops 19675488 | bytes 69811696 | tf_op jit(solution)/shard_map/convert_element_type | solution.py:356
  825.9 259.0 %while.65 = (s32[]{:T(128)}, f32[266,1536]{1,0:T(8,128)}, f32[133,16,96]{2,0,1:T(8,128)}, f32[16,6,11]{0,2,1:T(8,128)S(1)}, s32[133]{0:T(256)S(1)}, /*index=5*/s...) while((s32[]{:T(128)}, f32[266,1536]{1,0:T(8,128)}, ...), condition=%wide.region_149.150_spmd.clone, body=%wide.region_82.149_spmd.clone.sunk | while | flops 246337056 | bytes 252834448 | solution.py:382
  900.7 41.3 %select_convert_fusion.3 = bf16[16,133,138]{2,1,0:T(8,128)(2,1)S(1)} fusion(f32[16,128,128]{2,1,0:T(8,128)} %get-tuple-element.2008, f32[16,128,128]{2,1,0:T(8,128)} %get-tuple-element.2009, f32[16,128,128]{2,1,0:T(8,128)} %get-tuple-element.2010, f32[16,128,128]{2,1,0:T(8,128)} %get-tuple-element.2011, f32[16,128,128]{2,1,0:T(8,128)} %get-tuple-element.2012, ...), kind=kLoop, calls=%fused_computation.215.clone.1 | loop fusion | flops 19675488 | bytes 69811696 | tf_op jit(solution)/shard_map/while/body/eval_jaxpr/convert_element_type | solution.py:356
  1024.1 41.1 %select_convert_fusion.3 = bf16[16,133,138]{2,1,0:T(8,128)(2,1)S(1)} fusion(f32[16,128,128]{2,1,0:T(8,128)} %get-tuple-element.2008, f32[16,128,128]{2,1,0:T(8,128)} %get-tuple-element.2009, f32[16,128,128]{2,1,0:T(8,128)} %get-tuple-element.2010, f32[16,128,128]{2,1,0:T(8,128)} %get-tuple-element.2011, f32[16,128,128]{2,1,0:T(8,128)} %get-tuple-element.2012, ...), kind=kLoop, calls=%fused_computation.215.clone.1 | loop fusion | flops 19675488 | bytes 69811696 | tf_op jit(solution)/shard_map/while/body/eval_jaxpr/convert_element_type | solution.py:356
  1154.1 32.6 %fusion.155 = f32[8,2,2,1,1]{2,1,4,3,0:T(2,128)S(1)} fusion(f32[3,8,2,128,128]{3,2,0,4,1:T(2,128)} %copy.122, f32[3,8,2,128,128]{3,4,0,2,1:T(8,128)} %bitcast.1431), kind=kOutput, calls=%fused_computation.515 | convolution fusion | flops 18874368 | bytes 6291584 | tf_op jit(solution)/shard_map/rgdtk,rgctk->gcd/dot_general | solution.py:330
  1198.8 44.1 %all-reduce.273 = (f32[1536]{0:T(1024)S(1)}, f32[1536]{0:T(1024)S(1)}, f32[1536]{0:T(1024)S(1)}, f32[16,6,11]{0,1,2:T(8,128)}, f32[16,2]{0,1:T(2,128)}) all-reduce(f32[1536]{0:T(1024)S(1)} %get-tuple-element.966, f32[1536]{0:T(1024)S(1)} %reshape.1400, ...), channel_id=9, replica_groups=mesh['seq'=4,'wide'=8] {'seq','wide'}, use_global_device_ids=true, to_apply=%region_156.157.clone | all-reduce | flops 5696 | bytes 45568
  1246.8 124.9 %reduce-scatter.18.cloned.1.call-done = f32[48,1536]{1,0:T(8,128)} async-done(((f32[1536,1536]{1,0:T(8,128)}), f32[48,1536]{1,0:T(8,128)}) %reduce-scatter.18.cloned.1.call-update) | async-done | bytes 294928 | tf_op jit(solution)/shard_map/reduce_scatter | solution.py:423
  1371.7 140.9 %reduce-scatter.16.cloned.1.call-done = f32[48,1536]{1,0:T(8,128)} async-done(((f32[1536,1536]{1,0:T(8,128)}), f32[48,1536]{1,0:T(8,128)}) %reduce-scatter.16.cloned.1.call-update) | async-done | bytes 294928 | tf_op jit(solution)/shard_map/reduce_scatter | solution.py:422
  (1000 shorter events, 477.3 us)
Async XLA Ops:
  7.2 70.9 %all-gather.13.cloned.1.call-start = ((), (), s32[]{:S(2)}) async-start(), calls=%async_computation.10 | async-start | bytes 4866048 | tf_op jit(solution)/shard_map/all_gather | solution.py:128
  9.0 135.2 %all-gather.11.cloned.1.call-start = ((), (), s32[]{:S(2)}) async-start(), calls=%async_computation.9 | async-start | bytes 4866048 | tf_op jit(solution)/shard_map/all_gather | solution.py:127
  10.8 199.5 %all-gather.15.cloned.1.call-start = ((), (), s32[]{:S(2)}) async-start(), calls=%async_computation.11 | async-start | bytes 4866048 | tf_op jit(solution)/shard_map/all_gather | solution.py:129
  12.5 319.7 %all-gather.17.cloned.1.call-start = ((), (), s32[]{:S(2)}) async-start(), calls=%async_computation.12 | async-start | bytes 4866048 | tf_op jit(solution)/shard_map/all_gather | solution.py:130
  14.2 325.9 %all-gather.23.cloned.1.call-start = ((), (), s32[]{:S(2)}) async-start(), calls=%async_computation.15 | async-start | bytes 1966080 | tf_op jit(solution)/shard_map/all_gather | solution.py:256
  15.1 396.8 %all-gather.19.cloned.1.call-start = ((), (), s32[]{:S(2)}) async-start(), calls=%async_computation.13 | async-start | bytes 3538944 | tf_op jit(solution)/shard_map/all_gather | solution.py:253
  147.4 66.0 %collective-permute-start.2 = (bf16[2,5,1536]{2,1,0:T(8,128)(2,1)S(1)}, bf16[2,5,1536]{2,1,0:T(8,128)(2,1)S(1)}, u32[]{:S(2)}, u32[]{:S(2)}) collective-permute-start(bf16[2,5,1536]{2,1,0:T(8,128)(2,1)S(1)} %get-tuple-element.1354), channel_id=1, source_target_pairs={{0,8},{8,16},{16,24},{1,9},{9,17},{17,25},{2,10},{10,18},{18,26},{... | collective-permute-start | bytes 92168 | tf_op jit(solution)/shard_map/ppermute | solution.py:28
  149.6 64.6 %collective-permute-start.3 = (bf16[2,5,1536]{2,1,0:T(8,128)(2,1)S(1)}, bf16[2,5,1536]{2,1,0:T(8,128)(2,1)S(1)}, u32[]{:S(2)}, u32[]{:S(2)}) collective-permute-start(bf16[2,5,1536]{2,1,0:T(8,128)(2,1)S(1)} %get-tuple-element.1355), channel_id=1, source_target_pairs={{8,0},{16,8},{24,16},{9,1},{17,9},{25,17},{10,2},{18,10},{26,18},{... | collective-permute-start | bytes 92168 | tf_op jit(solution)/shard_map/ppermute | solution.py:31
  222.1 13.7 collective-permute-start
  337.3 95.0 %all-gather.21.cloned.1.call-start = ((), (), s32[]{:S(2)}) async-start(), calls=%async_computation.14 | async-start | bytes 1966080 | tf_op jit(solution)/shard_map/all_gather | solution.py:255
  338.2 115.3 %all-gather.25.cloned.1.call-start = ((), (), s32[]{:S(2)}) async-start(), calls=%async_computation.16 | async-start | bytes 1966080 | tf_op jit(solution)/shard_map/all_gather | solution.py:257
  339.1 177.1 %all-gather.27.cloned.1.call-start = ((), (), s32[]{:S(2)}) async-start(), calls=%async_computation.25 | async-start | bytes 3538944 | tf_op jit(solution)/shard_map/all_gather | solution.py:270
  339.8 262.4 %reduce-scatter.14.cloned.1.call-start = ((), (), s32[]{:S(2)}) async-start(), calls=%async_computation.18 | async-start | bytes 3538944 | tf_op jit(solution)/shard_map/reduce_scatter | solution.py:280
  529.1 150.3 %reduce-scatter.12.cloned.1.call-start = ((), (), s32[]{:S(2)}) async-start(), calls=%async_computation.17 | async-start | bytes 3538944 | tf_op jit(solution)/shard_map/reduce_scatter | solution.py:262
  535.2 612.7 %reduce-scatter.28.cloned.1.call-start = ((), (), s32[]{:S(2)}) async-start(), calls=%async_computation.26 | async-start | bytes 1966080
  541.0 609.1 %reduce-scatter.26.cloned.1.call-start = ((), (), s32[]{:S(2)}) async-start(), calls=%async_computation.24 | async-start | bytes 1966080 | tf_op jit(solution)/shard_map/reduce_scatter | solution.py:292
  546.2 605.8 %reduce-scatter.24.cloned.1.call-start = ((), (), s32[]{:S(2)}) async-start(), calls=%async_computation.23 | async-start | bytes 1966080 | tf_op jit(solution)/shard_map/reduce_scatter | solution.py:289
  558.9 687.9 %reduce-scatter.22.cloned.1.call-start = ((), (), s32[]{:S(2)}) async-start(), calls=%async_computation.22 | async-start | bytes 9732096 | tf_op jit(solution)/shard_map/reduce_scatter | solution.py:425
  821.6 425.3 %reduce-scatter.20.cloned.1.call-start = ((), (), s32[]{:S(2)}) async-start(), calls=%async_computation.21 | async-start | bytes 9732096 | tf_op jit(solution)/shard_map/reduce_scatter | solution.py:424
  832.6 118.7 %collective-permute-start.1 = (bf16[266,1536]{1,0:T(8,128)(2,1)}, bf16[266,1536]{1,0:T(8,128)(2,1)}, u32[]{:S(2)}, u32[]{:S(2)}) collective-permute-start(bf16[266,1536]{1,0:T(8,128)(2,1)} %convert_element_type.446), channel_id=1, source_target_pairs={{8,0},{16,8},{24,16},{9,1},{17,9},{25,17},{10,2},{18,10},{26,18},{... | collective-permute-start | bytes 2451464 | tf_op jit(solution)/shard_map/while/body/eval_jaxpr/ppermute | solution.py:20
  956.5 118.0 %collective-permute-start.1 = (bf16[266,1536]{1,0:T(8,128)(2,1)}, bf16[266,1536]{1,0:T(8,128)(2,1)}, u32[]{:S(2)}, u32[]{:S(2)}) collective-permute-start(bf16[266,1536]{1,0:T(8,128)(2,1)} %convert_element_type.446), channel_id=1, source_target_pairs={{8,0},{16,8},{24,16},{9,1},{17,9},{25,17},{10,2},{18,10},{26,18},{... | collective-permute-start | bytes 2451464 | tf_op jit(solution)/shard_map/while/body/eval_jaxpr/ppermute | solution.py:20
  1092.6 279.2 %reduce-scatter.18.cloned.1.call-start = ((), (), s32[]{:S(2)}) async-start(), calls=%async_computation.20 | async-start | bytes 9732096 | tf_op jit(solution)/shard_map/reduce_scatter | solution.py:423
  1095.0 9.7 collective-permute-start.4
  1129.6 383.1 %reduce-scatter.16.cloned.1.call-start = ((), (), s32[]{:S(2)}) async-start(), calls=%async_computation.19 | async-start | bytes 9732096 | tf_op jit(solution)/shard_map/reduce_scatter | solution.py:422
  (325 other events, 2556.3 us)
Sparse Core Ops, SparseCore 0:
  11.6 66.5 all-gather.12
  81.7 62.5 all-gather.10
  147.7 62.4 all-gather.14
  213.6 63.9 all-gather.16
  279.5 18.4 all-gather.22
  337.4 74.3 all-gather.18
  414.0 18.2 all-gather.20
  433.8 19.6 all-gather.24
  455.7 60.4 all-gather.26
  529.3 72.8 reduce-scatter.13
  605.8 73.5 reduce-scatter.11
  681.8 27.3 reduce-scatter.27
  711.9 28.1 reduce-scatter.25
  742.5 28.1 reduce-scatter.23
  821.2 135.1 reduce-scatter.21
  1092.7 137.0 reduce-scatter.19
  1237.1 134.5 reduce-scatter.17
  1378.1 134.5 reduce-scatter.15
where the time goes:
time: 1530 us; the launch traced here: 1520 us
  waiting for transfers between devices  693 us (45%)
  other arithmetic  408 us (27%)
  matrix products  142 us (9%)
  local copies, waits for them, and re-layouts  124 us (8%)
  blocking collectives  86.3 us (6%)
  starting transfers between devices  26.3 us (2%)
  loops' own time  22.4 us (1%)
  between operations  17.2 us (1%)
    reduce_scatter x1, waiting for transfers between devices, shards(): lax.psum_scatter(grad_query_w, ('seq', 'wide'), scatter_dimension=0, tile...  141 us
    reduce_scatter x1, waiting for transfers between devices, shards(): lax.psum_scatter(grad_key_w, ('seq', 'wide'), scatter_dimension=0, tiled=...  125 us
    convert_element_type x3, other arithmetic, tile_grads(): grad_scores_b = grad_scores.astype(jnp.bfloat16)  125 us
    reduce_sum x17, other arithmetic, convolve(): kernel[:, shift_q, shift_k][:, None, None] * piece_view  88.2 us
    unnamed x2, blocking collectives  86.3 us
    mul x13, other arithmetic, convolve(): kernel[:, shift_q, shift_k][:, None, None] * piece_view  74.2 us
    reduce_scatter x1, waiting for transfers between devices, shards(): lax.psum_scatter(jnp.dot(hidden, down_mat, preferred_element_type=jnp.flo...  73.9 us
    all_gather x1, waiting for transfers between devices, shards(): ffn_all = lax.all_gather(ffn_in, 'wide', axis=0, tiled=True)  71.7 us
  transfers between devices with their start and end apart: 26, of which 13 were waited for; matrix products, arithmetic and copies ran while one was open for 42% of the time, Pallas kernels for 0%

commit v1 on v0

--- a/solution.py
+++ b/solution.py
@@ -1,6 +1,10 @@
+import functools
+
 import jax
 import jax.numpy as jnp
 from jax import lax
+from jax.experimental import pallas as pl
+from jax.experimental.pallas import tpu as pltpu
 from jax.sharding import PartitionSpec as P
 
 HEADS = 16
@@ -8,6 +12,9 @@
 CQ = 6
 CK = 11
 GROUP = 2
+LANES = 128
+BLOCK = 128
+RIM = 16
 
 
 precise = lax.Precision.HIGHEST
@@ -448,9 +455,754 @@
     )
 
 
+def dot_plain(left, right):
+    return lax.dot_general(left, right, (((1,), (0,)), ((), ())), preferred_element_type=jnp.float32)
+
+
+def dot_nt(left, right):
+    return lax.dot_general(left, right, (((1,), (1,)), ((), ())), preferred_element_type=jnp.float32)
+
+
+def dot_tn(left, right):
+    return lax.dot_general(left, right, (((0,), (0,)), ((), ())), preferred_element_type=jnp.float32)
+
+
+def halves(value):
+    high = value.astype(jnp.bfloat16)
+    return high, (value - high.astype(jnp.float32)).astype(jnp.bfloat16)
+
+
+def spread_lanes(tile, count):
+    return tile if count == 1 else jnp.concatenate([tile] * count, axis=1)
+
+
+def allowed_mask(starts, block, first_col, count):
+    cols = lax.broadcasted_iota(jnp.int32, (BLOCK, count * LANES), 1) + first_col
+    rows = lax.broadcasted_iota(jnp.int32, (BLOCK, count * LANES), 0) + block * BLOCK
+    return (cols >= spread_lanes(starts, count)) & (cols <= rows)
+
+
+def head_stats(values):
+    lane = lax.broadcasted_iota(jnp.int32, values.shape, 1)
+    mean = jnp.sum(values, axis=-1, keepdims=True) * (1.0 / HEAD_DIM)
+    center = jnp.where(lane < HEAD_DIM, values - mean, 0.0)
+    spread = jnp.sum(center * center, axis=-1, keepdims=True) * (1.0 / HEAD_DIM)
+    inverse = lax.rsqrt(spread + epsilon)
+    return center * inverse, inverse
+
+
+def forward_kernel(
+    blocks, reach, mix_ref, q_ref, k_ref, v_ref, start_ref, th_ref, tl_ref, gain_ref,
+    probs_ref, high_ref, att_ref, grouped_ref, low_ref, part_ref,
+):
+    key_rim = CK // 2
+    scaling = HEAD_DIM ** (-0.5)
+    for h in range(GROUP):
+        lanes = slice(h * LANES, (h + 1) * LANES)
+        high_ref[0, h, :RIM, :] = jnp.zeros((RIM, high_ref.shape[3]), jnp.bfloat16)
+        low_ref[h, :RIM, :] = jnp.zeros((RIM, high_ref.shape[3]), jnp.bfloat16)
+        for n in range(blocks):
+            first, last = max(0, n - reach), min(n + 3, blocks + 1)
+            rows = slice(n * BLOCK, (n + 1) * BLOCK)
+            scores = (
+                dot_nt(q_ref[0, rows, lanes], k_ref[0, first * BLOCK : last * BLOCK, lanes]) * scaling
+            )
+            keep = allowed_mask(start_ref[0, rows, :], n, first * BLOCK - key_rim, last - first)
+            high, low = halves(jnp.where(keep, scores, 0.0))
+            into = slice(RIM + n * BLOCK, RIM + (n + 1) * BLOCK)
+            cols = slice(first * LANES, last * LANES)
+            high_ref[0, h, into, cols] = high
+            low_ref[h, into, cols] = low
+    for n in range(blocks):
+        first = max(0, n - reach)
+        count = n - first + 1
+        rows = slice(n * BLOCK, (n + 1) * BLOCK)
+        starts = start_ref[0, rows, :]
+        offset = lax.broadcasted_iota(jnp.int32, (BLOCK, LANES), 0) + n * BLOCK - starts
+        keep = allowed_mask(starts, n, first * BLOCK, count)
+        window = slice((reach + 1 - count) * LANES, (reach + 1) * LANES)
+        probs = []
+        for h in range(GROUP):
+            pieces = []
+            for m in range(first, n + 1):
+                rim_rows = slice(n * BLOCK, (n + 1) * BLOCK + RIM)
+                cols = slice(m * LANES, (m + 2) * LANES)
+                high = high_ref[0, h, rim_rows, cols]
+                low = low_ref[h, rim_rows, cols]
+                part = (
+                    dot_plain(high, th_ref[h])
+                    + dot_plain(low, th_ref[h])
+                    + dot_plain(high, tl_ref[h])
+                )
+                for a in range(CQ):
+                    part_ref[a] = part[:, a * LANES : (a + 1) * LANES]
+                total = part_ref[0, RIM:, :]
+                for a in range(1, CQ):
+                    total = total + jnp.where(
+                        offset >= a, part_ref[a, RIM - a : RIM - a + BLOCK, :], 0.0
+                    )
+                pieces.append(total)
+            logits = pieces[0] if count == 1 else jnp.concatenate(pieces, axis=1)
+            logits = jnp.where(keep, logits, -jnp.inf)
+            peak = jnp.max(logits, axis=-1, keepdims=True)
+            raised = jnp.exp(logits - peak)
+            prob = raised / jnp.sum(raised, axis=-1, keepdims=True)
+            probs_ref[0, h, rows, window] = prob
+            probs.append(prob)
+        keys = slice(first * BLOCK, (n + 1) * BLOCK)
+        for h in range(GROUP):
+            lanes = slice(h * LANES, (h + 1) * LANES)
+            mixed = (mix_ref[h, 0] * probs[0] + mix_ref[h, 1] * probs[1]).astype(jnp.bfloat16)
+            attended = dot_plain(mixed, v_ref[0, keys, lanes])
+            att_ref[0, rows, lanes] = attended
+            normal, _ = head_stats(attended)
+            grouped_ref[0, rows, lanes] = (normal * gain_ref[:, lanes]).astype(jnp.bfloat16)
+
+
+def fold_rows(value):
+    return jnp.sum(value.reshape(value.shape[0] // 8, 8, value.shape[1]), axis=0)
+
+
+def backward_kernel(
+    blocks, reach, mix_ref, gg_ref, att_ref, gain_ref, q_ref, k_ref, v_ref, start_ref, stop_ref,
+    probs_ref, high_ref, th_ref, tl_ref,
+    dq_ref, dk_ref, dv_ref, taps_ref, mixg_ref, gaing_ref,
+    grad_ref, cross_ref, keyg_ref, valueg_ref,
+):
+    key_rim = CK // 2
+    scaling = HEAD_DIM ** (-0.5)
+
+    @pl.when(pl.program_id(0) == 0)
+    def _():
+        cross_ref[...] = jnp.zeros_like(cross_ref)
+        mixg_ref[...] = jnp.zeros_like(mixg_ref)
+        gaing_ref[...] = jnp.zeros_like(gaing_ref)
+
+    grad_ref[...] = jnp.zeros_like(grad_ref)
+    keyg_ref[...] = jnp.zeros_like(keyg_ref)
+    valueg_ref[...] = jnp.zeros_like(valueg_ref)
+    lane = lax.broadcasted_iota(jnp.int32, (BLOCK, LANES), 1)
+    for n in range(blocks):
+        first = max(0, n - reach)
+        count = n - first + 1
+        rows = slice(n * BLOCK, (n + 1) * BLOCK)
+        keys = slice(first * BLOCK, (n + 1) * BLOCK)
+        window = slice((reach + 1 - count) * LANES, (reach + 1) * LANES)
+        probs = [probs_ref[0, h, rows, window] for h in range(GROUP)]
+        mixed_grads = []
+        for h in range(GROUP):
+            lanes = slice(h * LANES, (h + 1) * LANES)
+            normal, inverse = head_stats(att_ref[0, rows, lanes])
+            grad_grouped = gg_ref[0, rows, lanes]
+            gaing_ref[:, lanes] += fold_rows(grad_grouped * normal)
+            scaled = jnp.where(lane < HEAD_DIM, grad_grouped * gain_ref[:, lanes], 0.0)
+            mean_one = jnp.sum(scaled, axis=-1, keepdims=True) * (1.0 / HEAD_DIM)
+            mean_two = jnp.sum(scaled * normal, axis=-1, keepdims=True) * (1.0 / HEAD_DIM)
+            grad_att = inverse * (scaled - mean_one - normal * mean_two)
+            grad_att = jnp.where(lane < HEAD_DIM, grad_att, 0.0).astype(jnp.bfloat16)
+            mixed_grads.append(dot_nt(grad_att, v_ref[0, keys, lanes]))
+            mixed = (mix_ref[h, 0] * probs[0] + mix_ref[h, 1] * probs[1]).astype(jnp.bfloat16)
+            valueg_ref[keys, lanes] += dot_tn(mixed, grad_att)
+        for h in range(GROUP):
+            for d in range(GROUP):
+                product = fold_rows(probs[d] * mixed_grads[h])
+                total = product[:, :LANES]
+                for m in range(1, count):
+                    total = total + product[:, m * LANES : (m + 1) * LANES]
+                mixg_ref[h * GROUP + d] += total
+        for d in range(GROUP):
+            grad_probs = mix_ref[0, d] * mixed_grads[0] + mix_ref[1, d] * mixed_grads[1]
+            delta = jnp.sum(probs[d] * grad_probs, axis=-1, keepdims=True)
+            grad_logits = probs[d] * (grad_probs - delta)
+            for m in range(count):
+                grad_ref[d, first + m, rows, :] = grad_logits[:, m * LANES : (m + 1) * LANES]
+    for h in range(GROUP):
+        lanes = slice(h * LANES, (h + 1) * LANES)
+        for n in range(blocks):
+            first, last = max(0, n - reach), min(n + 1, blocks - 1)
+            rows = slice(n * BLOCK, (n + 1) * BLOCK)
+            room = stop_ref[0, rows, :] - (
+                lax.broadcasted_iota(jnp.int32, (BLOCK, LANES), 0) + n * BLOCK
+            )
+            count = n + 2 - first
+            sums = [None] * (count + 1)
+            for m in range(first, last + 1):
+                highs, lows = [], []
+                for a in range(CQ):
+                    piece = grad_ref[h, m, n * BLOCK + a : (n + 1) * BLOCK + a, :]
+                    if a:
+                        piece = jnp.where(room > a, piece, 0.0)
+                    high, low = halves(piece)
+                    highs.append(high)
+                    lows.append(low)
+                high = jnp.concatenate(highs, axis=1)
+                low = jnp.concatenate(lows, axis=1)
+                part = (
+                    dot_nt(high, th_ref[h]) + dot_nt(low, th_ref[h]) + dot_nt(high, tl_ref[h])
+                )
+                for side in range(2):
+                    place = m - first + side
+                    value = part[:, side * LANES : (side + 1) * LANES]
+                    sums[place] = value if sums[place] is None else sums[place] + value
+                scores = high_ref[
+                    0, h, RIM + n * BLOCK : RIM + (n + 1) * BLOCK, m * LANES : (m + 2) * LANES
+                ]
+                if m <= n:
+                    cross_ref[h] += dot_tn(scores, high)
+                else:
+                    cross_ref[h, :LANES, :] += dot_tn(scores[:, :LANES], high)
+            total = jnp.concatenate(sums[:count], axis=1)
+            keep = allowed_mask(start_ref[0, rows, :], n, first * BLOCK - key_rim, count)
+            grad_scores = jnp.where(keep, total, 0.0).astype(jnp.bfloat16)
+            cols = slice(first * BLOCK, (first + count) * BLOCK)
+            dq_ref[0, rows, lanes] = (
+                dot_plain(grad_scores, k_ref[0, cols, lanes]) * scaling
+            ).astype(jnp.bfloat16)
+            keyg_ref[h, cols, :] += dot_tn(grad_scores, q_ref[0, rows, lanes])
+        dk_ref[0, :, lanes] = (
+            keyg_ref[h, key_rim : key_rim + blocks * BLOCK, :] * scaling
+        ).astype(jnp.bfloat16)
+    dv_ref[0] = valueg_ref[...].astype(jnp.bfloat16)
+
+    @pl.when(pl.program_id(0) == pl.num_programs(0) - 1)
+    def _():
+        height = LANES + 2 * 8
+        shift = (
+            lax.broadcasted_iota(jnp.int32, (height, CQ * LANES), 1) % LANES
+            - lax.broadcasted_iota(jnp.int32, (height, CQ * LANES), 0)
+            + (CK - 1)
+        )
+        for h in range(GROUP):
+            cross = cross_ref[h, :height, :]
+            taps_ref[h] = jnp.zeros(taps_ref.shape[1:], jnp.float32)
+            for b in range(CK):
+                taps_ref[h, b : b + 1, :] = jnp.sum(
+                    jnp.where(shift == b, cross, 0.0), axis=0, keepdims=True
+                )
+
+
+def pack_spec(shape):
+    return pl.BlockSpec((1,) + shape, lambda p: (p,) + (0,) * len(shape))
+
+
+def fixed_spec(shape):
+    return pl.BlockSpec(shape, lambda p: (0,) * len(shape))
+
+
+def attention_forward(mix, q, k, v, starts, table_high, table_low, gain, reach):
+    packs, length, width = q.shape
+    blocks = length // BLOCK
+    padded = k.shape[1]
+    return pl.pallas_call(
+        functools.partial(forward_kernel, blocks, reach),
+        grid=(packs,),
+        in_specs=[
+            pl.BlockSpec(memory_space=pltpu.SMEM),
+            pack_spec((length, width)),
+            pack_spec((padded, width)),
+            pack_spec((length, width)),
+            pack_spec((length, LANES)),
+            fixed_spec(table_high.shape),
+            fixed_spec(table_low.shape),
+            fixed_spec(gain.shape),
+        ],
+        out_specs=[
+            pack_spec((GROUP, length, (reach + 1) * LANES)),
+            pack_spec((GROUP, RIM + length, padded)),
+            pack_spec((length, width)),
+            pack_spec((length, width)),
+        ],
+        out_shape=[
+            jax.ShapeDtypeStruct((packs, GROUP, length, (reach + 1) * LANES), jnp.float32),
+            jax.ShapeDtypeStruct((packs, GROUP, RIM + length, padded), jnp.bfloat16),
+            jax.ShapeDtypeStruct((packs, length, width), jnp.float32),
+            jax.ShapeDtypeStruct((packs, length, width), jnp.bfloat16),
+        ],
+        scratch_shapes=[
+            pltpu.VMEM((GROUP, RIM + length, padded), jnp.bfloat16),
+            pltpu.VMEM((CQ, RIM + BLOCK, LANES), jnp.float32),
+        ],
+        compiler_params=pltpu.CompilerParams(vmem_limit_bytes=48 << 20),
+        name="attention_forward",
+    )(mix, q, k, v, starts, table_high, table_low, gain)
+
+
+def attention_backward(
+    mix, grad_grouped, attended, gain, q, k, v, starts, stops, probs, high, table_high, table_low, reach
+):
+    packs, length, width = q.shape
+    blocks = length // BLOCK
+    padded = k.shape[1]
+    return pl.pallas_call(
+        functools.partial(backward_kernel, blocks, reach),
+        grid=(packs,),
+        in_specs=[
+            pl.BlockSpec(memory_space=pltpu.SMEM),
+            pack_spec((length, width)),
+            pack_spec((length, width)),
+            fixed_spec(gain.shape),
+            pack_spec((length, width)),
+            pack_spec((padded, width)),
+            pack_spec((length, width)),
+            pack_spec((length, LANES)),
+            pack_spec((length, LANES)),
+            pack_spec((GROUP, length, (reach + 1) * LANES)),
+            pack_spec((GROUP, RIM + length, padded)),
+            fixed_spec(table_high.shape),
+            fixed_spec(table_low.shape),
+        ],
+        out_specs=[
+            pack_spec((length, width)),
+            pack_spec((length, width)),
+            pack_spec((length, width)),
+            fixed_spec((GROUP, 16, CQ * LANES)),
+            fixed_spec((GROUP * GROUP, 8, LANES)),
+            fixed_spec((8, width)),
+        ],
+        out_shape=[
+            jax.ShapeDtypeStruct((packs, length, width), jnp.bfloat16),
+            jax.ShapeDtypeStruct((packs, length, width), jnp.bfloat16),
+            jax.ShapeDtypeStruct((packs, length, width), jnp.bfloat16),
+            jax.ShapeDtypeStruct((GROUP, 16, CQ * LANES), jnp.float32),
+            jax.ShapeDtypeStruct((GROUP * GROUP, 8, LANES), jnp.float32),
+            jax.ShapeDtypeStruct((8, width), jnp.float32),
+        ],
+        scratch_shapes=[
+            pltpu.VMEM((GROUP, blocks, length + 8, LANES), jnp.float32),
+            pltpu.VMEM((GROUP, 2 * LANES, CQ * LANES), jnp.float32),
+            pltpu.VMEM((GROUP, padded, LANES), jnp.float32),
+            pltpu.VMEM((length, width), jnp.float32),
+        ],
+        compiler_params=pltpu.CompilerParams(vmem_limit_bytes=48 << 20),
+        name="attention_backward",
+    )(mix, grad_grouped, attended, gain, q, k, v, starts, stops, probs, high, table_high, table_low)
+
+
+def conv_tables(kernel):
+    heads = kernel.shape[0]
+    u = lax.broadcasted_iota(jnp.int32, (2 * LANES, CQ * LANES), 0)
+    j = lax.broadcasted_iota(jnp.int32, (2 * LANES, CQ * LANES), 1) % LANES
+    table = jnp.zeros((heads, 2 * LANES, CQ * LANES), jnp.float32)
+    for b in range(CK):
+        taps = jnp.repeat(kernel[:, :, b], LANES, axis=1)
+        table = jnp.where((j - u + CK - 1 == b)[None], taps[:, None, :], table)
+    return halves(table)
+
+
+FLAT = ("seq", "wide")
+
+
+def swapped(value, flip):
+    total = lax.axis_size("seq") * lax.axis_size("wide")
+    return lax.ppermute(value, FLAT, [(i, i ^ flip) for i in range(total)])
+
+
+class Place:
+    def __init__(self):
+        self.wide_count = lax.axis_size("wide")
+        self.depth = self.wide_count // 2
+        self.seq = lax.axis_index("seq")
+        wide = lax.axis_index("wide")
+        self.y = wide % 2
+        self.z = wide // 2
+        self.plane = 2 * self.seq + self.y
+        self.x_flip = 2 * self.wide_count
+        self.core_flip = self.wide_count
+        self.y_flip = 1
+        seqs = range(lax.axis_size("seq"))
+        self.plane_groups = [
+            [s * self.wide_count + z * 2 + y for s in seqs for y in range(2)] for z in range(self.depth)
+        ]
+        self.line_groups = [[z * 2 + y for z in range(self.depth)] for y in range(2)]
+
+
+CHIPS = (0, 4, 1, 5)
+
+
+def plane_gather(place, value):
+    near = [
+        value,
+        swapped(value, place.x_flip),
+        swapped(value, place.y_flip),
+        swapped(value, place.x_flip | place.y_flip),
+    ]
+    far = swapped(jnp.stack(near), place.core_flip)
+    parts = [None] * 8
+    for slot, k in enumerate(CHIPS):
+        parts[k] = near[slot]
+        parts[k | 2] = far[slot]
+    return jnp.stack(parts)
+
+
+def plane_scatter(place, terms):
+    kept = jnp.stack([terms[k] for k in CHIPS])
+    sent = jnp.stack([terms[k | 2] for k in CHIPS]).astype(jnp.bfloat16)
+    total = kept + swapped(sent, place.core_flip).astype(jnp.float32)
+    rounded = total.astype(jnp.bfloat16)
+    flips = (place.x_flip, place.y_flip, place.x_flip | place.y_flip)
+    result = total[0]
+    for slot, flip in enumerate(flips):
+        result = result + swapped(rounded[slot + 1], flip).astype(jnp.float32)
+    return result
+
+
+def plane_order(place, blocks):
+    return jnp.concatenate(
+        [lax.dynamic_slice_in_dim(blocks, i ^ place.plane, 1) for i in range(8)]
+    )
+
+
+def line_gather(place, value):
+    parts = jnp.stack([value] + [swapped(value, 2 * k) for k in range(1, place.depth)])
+    return jnp.concatenate(
+        [lax.dynamic_slice_in_dim(parts, i ^ place.z, 1) for i in range(place.depth)]
+    )
+
+
+def line_scatter(place, blocks):
+    total = lax.dynamic_index_in_dim(blocks, place.z, 0, keepdims=False)
+    sent = [
+        swapped(
+            lax.dynamic_index_in_dim(blocks, place.z ^ k, 0, keepdims=False).astype(jnp.bfloat16),
+            2 * k,
+        )
+        for k in range(1, place.depth)
+    ]
+    for part in sent:
+        total = total + part.astype(jnp.float32)
+    return total
+
+
+def plane_exchange(place, blocks):
+    return lax.all_to_all(blocks, FLAT, 0, 0, axis_index_groups=place.plane_groups)
+
+
+def out_rows_gathered(place, rows):
+    other = swapped(rows, place.y_flip)
+    pair = jnp.where(
+        place.y == 0, jnp.concatenate([rows, other]), jnp.concatenate([other, rows])
+    )
+    holds = place.z // 2 == place.y
+    moved = {}
+    for k in range(1, place.depth):
+        pairs = [
+            (s * place.wide_count + z * 2 + y, s * place.wide_count + (z ^ k) * 2 + y)
+            for s in range(lax.axis_size("seq"))
+            for z in range(place.depth)
+            for y in range(2)
+            if z // 2 == y
+        ]
+        moved[k] = lax.ppermute(pair, FLAT, pairs)
+    first = jnp.where(holds, pair, moved[2])
+    second = jnp.where(holds, moved[1], moved[3])
+    return jnp.where(place.z % 2 == 0, jnp.stack([first, second]), jnp.stack([second, first]))
+
+
+def out_rows_scattered(place, terms):
+    half = terms.shape[1] // 2
+    total = lax.dynamic_index_in_dim(terms, place.z % 2, 0, keepdims=False)
+    for k in range(1, place.depth):
+        pairs = [
+            (s * place.wide_count + z * 2 + y, s * place.wide_count + (z ^ k) * 2 + y)
+            for s in range(lax.axis_size("seq"))
+            for z in range(place.depth)
+            for y in range(2)
+            if (z ^ k) // 2 == y
+        ]
+        sent = lax.dynamic_index_in_dim(terms, (place.z ^ k) % 2, 0, keepdims=False)
+        total = total + lax.ppermute(sent.astype(jnp.bfloat16), FLAT, pairs).astype(jnp.float32)
+    holds = place.z // 2 == place.y
+    away = lax.dynamic_slice_in_dim(total, (1 - place.y) * half, half).astype(jnp.bfloat16)
+    pairs = [
+        (s * place.wide_count + z * 2 + z // 2, s * place.wide_count + z * 2 + 1 - z // 2)
+        for s in range(lax.axis_size("seq"))
+        for z in range(place.depth)
+    ]
+    got = lax.ppermute(away, FLAT, pairs).astype(jnp.float32)
+    return jnp.where(holds, lax.dynamic_slice_in_dim(total, place.y * half, half), got)
+
+
+def head_pad(count):
+    rows = jnp.arange(HEAD_DIM * count)
+    return jax.nn.one_hot(
+        rows // HEAD_DIM * LANES + rows % HEAD_DIM, LANES * count, dtype=jnp.bfloat16
+    )
+
+
+def split_columns(value):
+    half = value.shape[-2] // 2
+    rest = value[..., 4 * LANES :]
+    return value[..., : 4 * LANES], jnp.concatenate(
+        [rest[..., :half, :], rest[..., half:, :]], axis=-1
+    )
+
+
+def join_columns(main, rest):
+    half = LANES // 2
+    return jnp.concatenate(
+        [main, jnp.concatenate([rest[..., :half], rest[..., half:]], axis=-2)], axis=-1
+    )
+
+
+def plane_shards(
+    tokens, segments, w_query, w_key, w_value, w_out, gain_attn, gain_group, gain_ffn,
+    conv_kernel, head_mix, w_gate, w_up, w_down, cotangent,
+):
+    place = Place()
+    seq_count = lax.axis_size("seq")
+    depth = place.depth
+    count = tokens.shape[1]
+    length = count * seq_count
+    width = tokens.shape[2]
+    slab = w_query.shape[0]
+    reach = (length // 2 - 1) // BLOCK + 1
+    heads_width = GROUP * LANES
+    cols = GROUP * HEAD_DIM
+    bf16 = jnp.bfloat16
+    f32 = jnp.float32
+
+    stacked = jnp.stack([w_query, w_key, w_value]).astype(bf16)
+    stacked = stacked.reshape(3, slab, 8, cols).transpose(2, 1, 0, 3).reshape(8, slab, 3 * cols)
+    main, rest = split_columns(stacked)
+    gains_own = jnp.stack([gain_attn, gain_group, gain_ffn]).astype(bf16)
+    gains_own = jnp.pad(gains_own, ((0, 5), (0, LANES - slab)))
+    rest = jnp.concatenate([rest, jnp.broadcast_to(gains_own[None], (8, 8, LANES))], axis=1)
+    main, rest = plane_exchange(place, main), plane_exchange(place, rest)
+    main, rest = line_gather(place, main), line_gather(place, rest)
+
+    def by_rows(value):
+        tail = value.shape[2:]
+        value = value.reshape((depth, seq_count, 2) + tail)
+        return jnp.swapaxes(value, 0, 1)
+
+    main, rest = by_rows(main), by_rows(rest)
+    gains = rest[:, :, :, slab // 2 :, :]
+    gains = gains[..., :3, :slab].transpose(3, 0, 1, 2, 4).reshape(3, width).astype(f32)
+    table = join_columns(main, rest[:, :, :, : slab // 2, :]).reshape(width, 3 * cols)
+    w_attn = jnp.dot(table, head_pad(3 * GROUP), preferred_element_type=f32).astype(bf16)
+
+    own_tokens = tokens[0]
+    token_blocks = plane_order(place, plane_gather(place, own_tokens))
+
+    def by_pack(blocks):
+        return jnp.swapaxes(blocks.reshape((seq_count, 2) + blocks.shape[1:]), 0, 1)
+
+    def by_plane(value):
+        blocks = value.reshape((2, seq_count, count) + value.shape[2:])
+        return jnp.swapaxes(blocks, 0, 1).reshape((8, count) + value.shape[2:])
+
+    token_all = by_pack(token_blocks).reshape(2 * length, width)
+    inputs_all = token_all.astype(f32)
+    scale_all = lax.rsqrt(jnp.mean(inputs_all * inputs_all, axis=-1, keepdims=True) + epsilon)
+    normed = (inputs_all * scale_all * gains[0]).astype(bf16)
+
+    other_row = swapped(segments, place.y_flip)
+    seg = jnp.where(
+        place.y == 0,
+        jnp.concatenate([segments, other_row]),
+        jnp.concatenate([other_row, segments]),
+    )
+    starts = jnp.sum(seg[:, None, :] < seg[:, :, None], axis=-1, dtype=jnp.int32)
+    stops = jnp.sum(seg[:, None, :] <= seg[:, :, None], axis=-1, dtype=jnp.int32)
+    starts = jnp.broadcast_to(starts[:, :, None], (2, length, LANES))
+    stops = jnp.broadcast_to(stops[:, :, None], (2, length, LANES))
+    taps = lax.dynamic_slice_in_dim(conv_kernel, place.plane * GROUP, GROUP)
+    mix = lax.dynamic_slice_in_dim(head_mix, place.plane * GROUP, GROUP)
+    table_high, table_low = conv_tables(taps)
+    gain_heads = lax.dynamic_slice_in_dim(gains[1], place.plane * cols, cols)
+    gain_heads = jnp.pad(gain_heads.reshape(GROUP, HEAD_DIM), ((0, 0), (0, LANES - HEAD_DIM)))
+    gain_heads = gain_heads.reshape(1, heads_width)
+
+    sub = w_gate.shape[1] // seq_count
+    deep = w_gate.shape[0]
+    parts = deep // LANES
+    ffn_own = jnp.stack(
+        [
+            w_gate.astype(bf16).reshape(deep, seq_count, sub).swapaxes(0, 1),
+            w_up.astype(bf16).reshape(deep, seq_count, sub).swapaxes(0, 1),
+            w_down.astype(bf16)
+            .reshape(seq_count, sub, parts, LANES)
+            .swapaxes(1, 2)
+            .reshape(seq_count, deep, sub),
+        ],
+        axis=1,
+    )
+    ffn_own = lax.all_to_all(ffn_own, "seq", 0, 0)
+    ffn_w = lax.all_gather(
+        ffn_own, "wide", axis=0, tiled=False, axis_index_groups=place.line_groups
+    )
+    hidden_units = depth * sub
+    w_gate_up = (
+        ffn_w[:, :, :2].transpose(1, 3, 2, 0, 4).reshape(width, 2 * hidden_units)
+    )
+    w_down_all = (
+        ffn_w[:, :, 2]
+        .reshape(depth, seq_count, parts, sub, LANES)
+        .transpose(0, 3, 1, 2, 4)
+        .reshape(hidden_units, width)
+    )
+    w_out_heads = out_rows_gathered(place, w_out.astype(bf16))
+    w_out_heads = jnp.pad(w_out_heads, ((0, 0), (0, LANES - HEAD_DIM), (0, 0)))
+    w_out_heads = w_out_heads.reshape(heads_width, width)
+    grad_out = cotangent[0]
+    cot_all = plane_gather(place, grad_out).reshape(8 * count, width)
+
+    qkv = jnp.dot(normed, w_attn, preferred_element_type=f32).astype(bf16)
+    qkv = qkv.reshape(2, length, 3 * heads_width)
+    queries = qkv[..., :heads_width]
+    keys = jnp.pad(
+        qkv[..., heads_width : 2 * heads_width], ((0, 0), (CK // 2, LANES - CK // 2), (0, 0))
+    )
+    values = qkv[..., 2 * heads_width :]
+    probs, high, attended, grouped = attention_forward(
+        mix, queries, keys, values, starts, table_high, table_low, gain_heads, reach
+    )
+    grouped_rel = plane_order(place, by_plane(grouped)).reshape(8 * count, heads_width)
+    branch = jnp.dot(grouped_rel, w_out_heads, preferred_element_type=f32)
+    middle = own_tokens.astype(f32) + plane_scatter(place, branch.reshape(8, count, width))
+
+    scale_mid = lax.rsqrt(jnp.mean(middle * middle, axis=-1, keepdims=True) + epsilon)
+    ffn_in = (middle * scale_mid * gains[2]).astype(bf16)
+    ffn_all = plane_gather(place, ffn_in).reshape(8 * count, width)
+    gate_up = jnp.dot(ffn_all, w_gate_up, preferred_element_type=f32)
+    gate, up = gate_up[:, :hidden_units], gate_up[:, hidden_units:]
+    grad_hidden = contract(cot_all, w_down_all, 1, 1)
+    sig = jax.nn.sigmoid(gate)
+    hidden = (gate * sig * up).astype(bf16)
+    grad_gate = (grad_hidden * up * sig * (1.0 + gate * (1.0 - sig))).astype(bf16)
+    grad_up = (grad_hidden * gate * sig).astype(bf16)
+    grad_gate_up = jnp.concatenate([grad_gate, grad_up], axis=1)
+    grad_ffn_in = plane_scatter(
+        place, contract(grad_gate_up, w_gate_up, 1, 1).reshape(8, count, width)
+    )
+    ffn_out = plane_scatter(
+        place, jnp.dot(hidden, w_down_all, preferred_element_type=f32).reshape(8, count, width)
+    )
+    output = (middle + ffn_out).astype(bf16)
+    grad_gain_ffn = jnp.sum(grad_ffn_in * middle * scale_mid, axis=0)
+    scaled = grad_ffn_in * gains[2]
+    grad_middle = grad_out.astype(f32) + (
+        scale_mid * scaled
+        - middle
+        * (scale_mid * scale_mid * scale_mid)
+        * jnp.mean(scaled * middle, axis=-1, keepdims=True)
+    )
+    grad_branch = grad_middle.astype(bf16)
+
+    grad_gu_w = contract(ffn_all, grad_gate_up, 0, 0).astype(bf16)
+    grad_gu_w = grad_gu_w.reshape(seq_count, deep, 2, depth, sub).transpose(3, 0, 2, 1, 4)
+    grad_down_w = contract(hidden, cot_all, 0, 0).astype(bf16)
+    grad_down_w = (
+        grad_down_w.reshape(depth, sub, seq_count, parts, LANES)
+        .transpose(0, 2, 3, 1, 4)
+        .reshape(depth, seq_count, 1, deep, sub)
+    )
+    ffn_g = lax.psum_scatter(
+        jnp.concatenate([grad_gu_w, grad_down_w], axis=2),
+        "wide",
+        scatter_dimension=0,
+        axis_index_groups=place.line_groups,
+    )
+    ffn_g = lax.all_to_all(ffn_g, "seq", 0, 0).astype(f32)
+    grad_w_gate = ffn_g[:, 0].swapaxes(0, 1).reshape(deep, seq_count * sub)
+    grad_w_up = ffn_g[:, 1].swapaxes(0, 1).reshape(deep, seq_count * sub)
+    grad_w_down = (
+        ffn_g[:, 2]
+        .reshape(seq_count, parts, sub, LANES)
+        .swapaxes(1, 2)
+        .reshape(seq_count * sub, deep)
+    )
+
+    branch_blocks = plane_order(place, plane_gather(place, grad_branch))
+    branch_all = by_pack(branch_blocks).reshape(2 * length, width)
+    grad_grouped = contract(branch_all, w_out_heads, 1, 1).reshape(2, length, heads_width)
+    grad_w_out = contract(grouped.reshape(2 * length, heads_width), branch_all, 0, 0)
+    grad_w_out = out_rows_scattered(
+        place, grad_w_out.reshape(GROUP, LANES, width)[:, :HEAD_DIM]
+    )
+    grad_q, grad_k, grad_v, grad_taps, grad_mix, grad_gain_group = attention_backward(
+        mix, grad_grouped, attended, gain_heads, queries, keys, values, starts, stops,
+        probs, high, table_high, table_low, reach,
+    )
+    grad_qkv = jnp.concatenate([grad_q, grad_k, grad_v], axis=-1)
+    grad_rel = plane_order(place, by_plane(grad_qkv)).reshape(8 * count, 3 * heads_width)
+    normed_part = contract(grad_rel, w_attn, 1, 1)
+    grad_normed = plane_scatter(place, normed_part.reshape(8, count, width))
+
+    grad_table = contract(normed, grad_qkv.reshape(2 * length, 3 * heads_width), 0, 0)
+    grad_table = contract(grad_table.astype(bf16), head_pad(3 * GROUP), 1, 1).astype(bf16)
+    grad_table = jnp.swapaxes(
+        grad_table.reshape(seq_count, depth, 2, slab, 3 * cols), 0, 1
+    ).reshape(depth, 8, slab, 3 * cols)
+    main, rest = split_columns(grad_table)
+    main = line_scatter(place, main.astype(f32)).astype(bf16)
+    rest = line_scatter(place, rest.astype(f32)).astype(bf16)
+    main, rest = plane_exchange(place, main), plane_exchange(place, rest)
+    grad_rows = join_columns(main, rest).reshape(8, slab, 3, cols).transpose(2, 1, 0, 3)
+    grad_rows = grad_rows.reshape(3, slab, width).astype(f32)
+
+    inputs = own_tokens.astype(f32)
+    scale_in = lax.rsqrt(jnp.mean(inputs * inputs, axis=-1, keepdims=True) + epsilon)
+    grad_gain_attn = jnp.sum(grad_normed * inputs * scale_in, axis=0)
+    scaled_in = grad_normed * gains[0]
+    grad_tokens = (
+        grad_middle
+        + scale_in * scaled_in
+        - inputs
+        * (scale_in * scale_in * scale_in)
+        * jnp.mean(scaled_in * inputs, axis=-1, keepdims=True)
+    ).astype(bf16)
+
+    tap_sums = grad_taps[:, :CK].reshape(GROUP, CK, CQ, LANES).sum(-1).swapaxes(1, 2)
+    mix_sums = grad_mix.sum((1, 2)).reshape(GROUP, GROUP)
+    group_sums = grad_gain_group.sum(0).reshape(GROUP, LANES)[:, :HEAD_DIM].reshape(cols)
+
+    def placed(value, full, start):
+        return lax.dynamic_update_slice_in_dim(jnp.zeros(full, f32), value, start, 0)
+
+    small = [
+        grad_gain_attn,
+        grad_gain_ffn,
+        placed(group_sums, (width,), place.plane * cols),
+        placed(tap_sums, (HEADS, CQ, CK), place.plane * GROUP).reshape(-1),
+        placed(mix_sums, (HEADS, GROUP), place.plane * GROUP).reshape(-1),
+    ]
+    sizes = [value.shape[0] for value in small]
+    flat = jnp.concatenate(small)
+    padded = -flat.shape[0] % (8 * LANES)
+    flat = jnp.pad(flat, (0, padded)).reshape(-1, LANES)
+    for flip in (place.core_flip, place.x_flip, place.y_flip, 2, 4):
+        flat = flat + swapped(flat, flip)
+    flat = flat.reshape(-1)
+    row = (place.seq * place.wide_count + lax.axis_index("wide")) * slab
+    gain_grads = [
+        lax.dynamic_slice_in_dim(flat, i * width + row, slab) for i in range(3)
+    ]
+    at = 3 * width
+    grad_conv = flat[at : at + sizes[3]].reshape(HEADS, CQ, CK)
+    grad_head_mix = flat[at + sizes[3] : at + sizes[3] + sizes[4]].reshape(HEADS, GROUP)
+    return (
+        output[None],
+        grad_tokens[None],
+        grad_rows[0],
+        grad_rows[1],
+        grad_rows[2],
+        grad_w_out,
+        gain_grads[0],
+        gain_grads[2],
+        gain_grads[1],
+        grad_conv,
+        grad_head_mix,
+        grad_w_gate,
+        grad_w_up,
+        grad_w_down,
+    )
+
+
 def solution(mesh):
+    planes = mesh.shape["seq"] == 4 and mesh.shape["wide"] == 8
     return jax.shard_map(
-        shards,
+        plane_shards if planes else shards,
         mesh=mesh,
         in_specs=(
             P("wide", "seq", None),

time: 1530 us -> 648 us (0.42)
  waiting for transfers between devices: 693 us -> 170 us
  other arithmetic: 408 us -> 71.9 us
  starting transfers between devices: 26.3 us -> 130 us
  matrix products: 142 us -> 52.8 us
  blocking collectives: 86.3 us -> 0 us
  Pallas kernels: 0 us -> 47.6 us
  local copies, waits for them, and re-layouts: 124 us -> 148 us
  loops' own time: 22.4 us -> 0 us
    reduce_scatter x8 -> x1, waiting for transfers between devices: 383 us -> 0.01 us  [plane_shards(): lax.psum_scatter(jnp.concatenate([grad_gu_w, grad_down_w], axis=2), 'wide...]
    all_gather x9 -> x1, waiting for transfers between devices: 305 us -> 28.6 us  [plane_shards(): lax.all_gather(ffn_own, 'wide', axis=0, tiled=False, axis_index_groups=pl...]
    ppermute x8 -> x58, waiting for transfers between devices: 3.83 us -> 141 us  [the longest x51 117 us: swapped(): return lax.ppermute(value, FLAT, [(i, i ^ flip) for i in range(total)])]
    convert_element_type x51 -> x18, other arithmetic: 149 us -> 23.7 us  [the longest x4 9.71 us: plane_scatter(): rounded = total.astype(jnp.bfloat16)]
    reduce_sum x24 -> x8, other arithmetic: 96.6 us -> 9.64 us  [the longest x1 4.26 us: plane_shards(): grad_gain_ffn = jnp.sum(grad_ffn_in * middle * scale_mid, axis=0)]
    unnamed x2 -> x0, blocking collectives: 86.3 us -> none
    ppermute x8 -> x58, starting transfers between devices: 24.9 us -> 105 us  [the longest x51 86.2 us: swapped(): return lax.ppermute(value, FLAT, [(i, i ^ flip) for i in range(total)])]
    mul x14 -> x2, other arithmetic: 75.5 us -> 0.53 us  [the longest x1 0.52 us: plane_shards(): scale_in * scale_in * scale_in]
  transfers between devices with their start and end apart: 26 -> 66, of which waited for: 13 -> 33; matrix products, arithmetic and copies ran while one was open for 42% -> 34% of each run, Pallas kernels for 0% -> 7%
where the time goes in v1:
time: 648 us; the launch traced here: 637 us
  waiting for transfers between devices  170 us (26%)
  local copies, waits for them, and re-layouts  148 us (23%)
  starting transfers between devices  130 us (20%)
  other arithmetic  71.9 us (11%)
  matrix products  52.8 us (8%)
  Pallas kernels  47.6 us (7%)
  between operations  16.5 us (3%)
    ppermute x51, waiting for transfers between devices, swapped(): return lax.ppermute(value, FLAT, [(i, i ^ flip) for i in range(total)])  117 us
    ppermute x51, starting transfers between devices, swapped(): return lax.ppermute(value, FLAT, [(i, i ^ flip) for i in range(total)])  86.2 us
    unnamed x213, local copies, waits for them, and re-layouts  52.8 us
    dot_general x8, matrix products, contract(): lax.dot_general(left_op, right_op, (((left_dim,), (right_dim,)), ((), ())...  35.9 us
    pallas_call x1, Pallas kernels, attention_backward(): pl.pallas_call(functools.partial(backward_kernel, blocks, reach), grid=(p...  32.4 us
    all_gather x1, waiting for transfers between devices, plane_shards(): lax.all_gather(ffn_own, 'wide', axis=0, tiled=False, axis_index_groups=pl...  28.6 us
    ppermute x3, waiting for transfers between devices, out_rows_scattered(): lax.ppermute(sent.astype(jnp.bfloat16), FLAT, pairs).astype(jnp.float32)  23.6 us
    all_to_all x4, starting transfers between devices, plane_exchange(): lax.all_to_all(blocks, FLAT, 0, 0, axis_index_groups=place.plane_groups)  17.5 us
  transfers between devices with their start and end apart: 66, of which 33 were waited for; matrix products, arithmetic and copies ran while one was open for 34% of the time, Pallas kernels for 7%

profile of v1, /device:TPU:0, one launch (start us, length us, event | category | flops | bytes accessed | tf_op | source)
XLA Modules:
  0.0 637.3 jit_solution(5525606346636874228)
XLA Ops:
  63.1 5.6 collective-permute-done.11
  74.7 6.2 collective-permute-start.14
  80.9 7.2 %collective-permute-done.27 = bf16[128,1536]{1,0:T(8,128)(2,1)S(1)} collective-permute-done((bf16[128,1536]{1,0:T(8,128)(2,1)S(1)}, bf16[128,1536]{1,0:T(8,128)(2,1)S(1)}, u32[]{:S(2)}, u32[]{:S(2)}) %collective-permute-start.27) | collective-permute-done | bytes 393248 | tf_op jit(solution)/shard_map/ppermute | solution.py:797
  105.1 20.6 %collective-permute-start.7 = (bf16[8,48,512]{2,1,0:T(8,128)(2,1)}, bf16[8,48,512]{2,1,0:T(8,128)(2,1)S(1)}, u32[]{:S(2)}, u32[]{:S(2)}) collective-permute-start(bf16[8,48,512]{2,1,0:T(8,128)(2,1)} %all-to-all-done.1), channel_id=1, source_target_pairs={{0,2},{1,3},{2,0},{3,1},{4,6},{5,7},{6,4},{7,5},{8,10},{9,11},{10,... | collective-permute-start | bytes 1179656 | tf_op jit(solution)/shard_map/ppermute | solution.py:797
  128.5 9.5 %collective-permute-done.8 = bf16[8,48,512]{2,1,0:T(8,128)(2,1)S(1)} collective-permute-done((bf16[8,48,512]{2,1,0:T(8,128)(2,1)}, bf16[8,48,512]{2,1,0:T(8,128)(2,1)S(1)}, u32[]{:S(2)}, u32[]{:S(2)}) %collective-permute-start.8) | collective-permute-done | bytes 393248 | tf_op jit(solution)/shard_map/ppermute | solution.py:797
  156.3 15.2 %attention_forward.1 = (f32[2,2,512,384]{3,2,1,0:T(8,128)}, bf16[2,2,528,640]{3,2,1,0:T(8,128)(2,1)}, f32[2,512,256]{2,1,0:T(8,128)S(1)}, bf16[2,512,256]{2,1,0:T(8,128)(2,1)S(1)}) custom-call(f32[2,2]{1,0:T(2,128)S(1)} %copy.300.mix_ref, bf16[2,512,256]{2,1,0:T(8,128)(2,1)S(1)} %get-tuple-element.186.q_ref, bf16[2,640,256]{2,1,0:T(8,128)(2,1)S(1)} %pad.21.k_ref, ...), custom_call_target="tpu_custom_call" | custom-call | tf_op jit(solution)/shard_map/attention_forward/pallas_call | solution.py:696
  194.1 6.2 collective-permute-done.16
  200.2 10.1 %collective-permute-done.18 = bf16[128,1536]{1,0:T(8,128)(2,1)S(1)} collective-permute-done((bf16[128,1536]{1,0:T(8,128)(2,1)S(1)}, bf16[128,1536]{1,0:T(8,128)(2,1)S(1)}, u32[]{:S(2)}, u32[]{:S(2)}) %collective-permute-start.18) | collective-permute-done | bytes 393248 | tf_op jit(solution)/shard_map/ppermute | solution.py:797
  218.1 8.7 %collective-permute-done.21 = bf16[128,1536]{1,0:T(8,128)(2,1)S(1)} collective-permute-done((bf16[128,1536]{1,0:T(8,128)(2,1)S(1)}, bf16[128,1536]{1,0:T(8,128)(2,1)S(1)}, u32[]{:S(2)}, u32[]{:S(2)}) %collective-permute-start.21) | collective-permute-done | bytes 393248 | tf_op jit(solution)/shard_map/ppermute | solution.py:797
  226.8 5.7 collective-permute-done.20
  243.7 28.6 %all-gather.3.cloned.1.call-done = bf16[16,3,384,128]{3,2,1,0:T(8,128)(2,1)} async-done(((bf16[4,3,384,128]{3,2,1,0:T(8,128)(2,1)}), bf16[16,3,384,128]{3,2,1,0:T(8,128)(2,1)}) %all-gather.3.cloned.1.call-update) | async-done | bytes 4718608 | tf_op jit(solution)/shard_map/all_gather | solution.py:1031
  280.8 6.1 reshape.952
  290.6 6.6 %fusion.112 = f32[1024,1024]{0,1:T(8,128)S(1)} fusion(bf16[1024,1536]{1,0:T(8,128)(2,1)} %bitcast.64, bf16[1536,1024]{1,0:T(8,128)(2,1)} %reshape.952), kind=kOutput, calls=%fused_computation.370 | convolution fusion | flops 3221225472 | bytes 10485760 | tf_op jit(solution)/shard_map/dot_general | solution.py:1067
  324.8 7.9 %collective-permute-done.34 = bf16[128,1536]{1,0:T(8,128)(2,1)} collective-permute-done((bf16[128,1536]{1,0:T(8,128)(2,1)}, bf16[128,1536]{1,0:T(8,128)(2,1)}, u32[]{:S(2)}, u32[]{:S(2)}) %collective-permute-start.34) | collective-permute-done | bytes 393248 | tf_op jit(solution)/shard_map/ppermute | solution.py:797
  335.0 5.2 collective-permute-done.24
  340.2 8.7 %collective-permute-done.26 = bf16[128,1536]{1,0:T(8,128)(2,1)} collective-permute-done((bf16[128,1536]{1,0:T(8,128)(2,1)}, bf16[128,1536]{1,0:T(8,128)(2,1)}, u32[]{:S(2)}, u32[]{:S(2)}) %collective-permute-start.26) | collective-permute-done | bytes 393248 | tf_op jit(solution)/shard_map/ppermute | solution.py:797
  369.4 5.1 collective-permute-done.36
  378.2 7.8 %convolution_convert_fusion = bf16[1536,1024]{1,0:T(8,128)(2,1)} fusion(bf16[1024,1536]{1,0:T(8,128)(2,1)} %bitcast.64, bf16[1024,512]{0,1:T(8,128)(2,1)S(1)} %copy-done.67, bf16[1024,512]{0,1:T(8,128)(2,1)S(1)} %copy-done.65), kind=kOutput, calls=%fused_computation.9 | convolution fusion | flops 3226992640 | bytes 8388608 | tf_op jit(solution)/shard_map/dot_general | solution.py:124
  385.9 6.1 reshape.973
  409.4 5.0 pad_maximum_fusion
  434.8 32.4 %attention_backward.1 = (bf16[2,512,256]{2,1,0:T(8,128)(2,1)S(1)}, bf16[2,512,256]{2,1,0:T(8,128)(2,1)S(1)}, bf16[2,512,256]{2,1,0:T(8,128)(2,1)S(1)}, f32[2,16,...) custom-call(f32[2,2]{1,0:T(2,128)S(1)} %copy.300.mix_ref, f32[2,512,256]{2,1,0:T(8,128)} %fusion.113.gg_ref, ...), custom_call_target="tpu_custom_call" | custom-call | tf_op jit(solution)/shard_map/attention_backward/pallas_call | solution.py:736
  479.9 8.9 %convolution_convert_fusion.3 = bf16[1536,576]{0,1:T(8,128)(2,1)} fusion(s32[576]{0:T(1024)S(1)} %copy-done.56, bf16[1024,1536]{1,0:T(8,128)(2,1)} %bitcast.500, bf16[1024,768]{1,0:T(8,128)(2,1)} %bitcast.502), kind=kOutput, calls=%fused_computation.18 | convolution fusion | flops 3777380352 | bytes 6490368 | tf_op jit(solution)/shard_map/dot_general | solution.py:124
  525.0 5.9 collective-permute-start.44
  530.9 23.6 %collective-permute-done.50 = bf16[96,1536]{1,0:T(8,128)(2,1)} collective-permute-done((bf16[96,1536]{1,0:T(8,128)(2,1)}, bf16[96,1536]{1,0:T(8,128)(2,1)}, u32[]{:S(2)}, u32[]{:S(2)}) %collective-permute-start.50) | collective-permute-done | bytes 294944 | tf_op jit(solution)/shard_map/ppermute | solution.py:913
  (542 shorter events, 368.0 us)
Async XLA Ops:
  7.2 91.9 %collective-permute-start.1 = (bf16[128,1536]{1,0:T(8,128)(2,1)}, bf16[128,1536]{1,0:T(8,128)(2,1)}, u32[]{:S(2)}, u32[]{:S(2)}) collective-permute-start(bf16[128,1536]{1,0:T(8,128)(2,1)} %bitcast.467), channel_id=1, source_target_pairs={{0,16},{1,17},{2,18},{3,19},{4,20},{5,21},{6,22},{7,23},{8,24},{9,... | collective-permute-start | bytes 1179656 | tf_op jit(solution)/shard_map/ppermute | solution.py:797
  10.2 61.3 %collective-permute-start = (bf16[128,1536]{1,0:T(8,128)(2,1)}, bf16[128,1536]{1,0:T(8,128)(2,1)}, u32[]{:S(2)}, u32[]{:S(2)}) collective-permute-start(bf16[128,1536]{1,0:T(8,128)(2,1)} %bitcast.468), channel_id=1, source_target_pairs={{0,1},{1,0},{2,3},{3,2},{4,5},{5,4},{6,7},{7,6},{8,9},{9,8},{10,11... | collective-permute-start | bytes 1179656 | tf_op jit(solution)/shard_map/ppermute | solution.py:797
  11.7 30.8 %collective-permute-start.10 = (s32[1,512]{1,0:T(1,128)}, s32[1,512]{1,0:T(1,128)S(1)}, u32[]{:S(2)}, u32[]{:S(2)}) collective-permute-start(s32[1,512]{1,0:T(1,128)} %param.16), channel_id=1, source_target_pairs={{0,1},{1,0},{2,3},{3,2},{4,5},{5,4},{6,7},{7,6},{8,9},{9,8},{10,11... | collective-permute-start | bytes 6152 | tf_op jit(solution)/shard_map/ppermute | solution.py:797
  42.6 52.2 %all-to-all-start.1 = ((bf16[8,48,512]{2,1,0:T(8,128)(2,1)}), bf16[8,48,512]{2,1,0:T(8,128)(2,1)}, u32[]{:S(2)}, u32[]{:S(2)}) async-start(bf16[8,48,512]{2,1,0:T(8,128)(2,1)} %slice.607), calls=%async_computation.1 | async-start | bytes 786432 | tf_op jit(solution)/shard_map/all_to_all | solution.py:877
  53.8 46.2 %collective-permute-start.2 = (bf16[128,1536]{1,0:T(8,128)(2,1)S(1)}, bf16[128,1536]{1,0:T(8,128)(2,1)}, u32[]{:S(2)}, u32[]{:S(2)}) collective-permute-start(bf16[128,1536]{1,0:T(8,128)(2,1)S(1)} %bitcast.469), channel_id=1, source_target_pairs={{0,17},{1,16},{2,19},{3,18},{4,21},{5,20},{6,23},{7,22},{8,25},{9,... | collective-permute-start | bytes 1179656 | tf_op jit(solution)/shard_map/ppermute | solution.py:797
  74.7 52.0 %collective-permute-start.14 = (bf16[96,1536]{1,0:T(8,128)(2,1)}, bf16[96,1536]{1,0:T(8,128)(2,1)}, u32[]{:S(2)}, u32[]{:S(2)}) collective-permute-start(bf16[96,1536]{1,0:T(8,128)(2,1)} %maximum_select_fusion.1), channel_id=1, source_target_pairs={{0,6},{2,4},{5,3},{7,1},{8,14},{10,12},{13,11},{15,9},{16,22},{18,... | collective-permute-start | bytes 884744 | tf_op jit(solution)/shard_map/ppermute | solution.py:895
  88.1 38.7 %collective-permute-start.13 = (bf16[96,1536]{1,0:T(8,128)(2,1)}, bf16[96,1536]{1,0:T(8,128)(2,1)}, u32[]{:S(2)}, u32[]{:S(2)}) collective-permute-start(bf16[96,1536]{1,0:T(8,128)(2,1)} %maximum_select_fusion.1), channel_id=1, source_target_pairs={{0,2},{2,0},{5,7},{7,5},{8,10},{10,8},{13,15},{15,13},{16,18},{18,... | collective-permute-start | bytes 884744 | tf_op jit(solution)/shard_map/ppermute | solution.py:895
  94.8 84.8 %all-to-all-start.2 = ((bf16[4,3,384,128]{2,3,1,0:T(8,128)(2,1)}), bf16[4,3,384,128]{2,3,1,0:T(8,128)(2,1)}, u32[]{:S(2)}, u32[]{:S(2)}) async-start(bf16[4,3,384,128]{2,3,1,0:T(8,128)(2,1)} %copy.272), calls=%async_computation.2 | async-start | bytes 2359296 | tf_op jit(solution)/shard_map/all_to_all | solution.py:1030
  99.1 173.2 %all-gather.3.cloned.1.call-start = ((), (), s32[]{:S(2)}) async-start(), calls=%async_computation.8 | async-start | bytes 5898240 | tf_op jit(solution)/shard_map/all_gather | solution.py:1031
  99.1 29.4 %collective-permute-start.9 = (bf16[8,48,512]{2,1,0:T(8,128)(2,1)}, bf16[8,48,512]{2,1,0:T(8,128)(2,1)S(1)}, u32[]{:S(2)}, u32[]{:S(2)}) collective-permute-start(bf16[8,48,512]{2,1,0:T(8,128)(2,1)} %all-to-all-done.1), channel_id=1, source_target_pairs={{0,6},{1,7},{2,4},{3,5},{4,2},{5,3},{6,0},{7,1},{8,14},{9,15},{10,... | collective-permute-start | bytes 1179656 | tf_op jit(solution)/shard_map/ppermute | solution.py:797
  100.0 37.9 %collective-permute-start.8 = (bf16[8,48,512]{2,1,0:T(8,128)(2,1)}, bf16[8,48,512]{2,1,0:T(8,128)(2,1)S(1)}, u32[]{:S(2)}, u32[]{:S(2)}) collective-permute-start(bf16[8,48,512]{2,1,0:T(8,128)(2,1)} %all-to-all-done.1), channel_id=1, source_target_pairs={{0,4},{1,5},{2,6},{3,7},{4,0},{5,1},{6,2},{7,3},{8,12},{9,13},{10,... | collective-permute-start | bytes 1179656 | tf_op jit(solution)/shard_map/ppermute | solution.py:797
  105.1 36.4 %collective-permute-start.7 = (bf16[8,48,512]{2,1,0:T(8,128)(2,1)}, bf16[8,48,512]{2,1,0:T(8,128)(2,1)S(1)}, u32[]{:S(2)}, u32[]{:S(2)}) collective-permute-start(bf16[8,48,512]{2,1,0:T(8,128)(2,1)} %all-to-all-done.1), channel_id=1, source_target_pairs={{0,2},{1,3},{2,0},{3,1},{4,6},{5,7},{6,4},{7,5},{8,10},{9,11},{10,... | collective-permute-start | bytes 1179656 | tf_op jit(solution)/shard_map/ppermute | solution.py:797
  126.8 55.4 %collective-permute-start.30 = (bf16[4,128,1536]{2,1,0:T(8,128)(2,1)}, bf16[4,128,1536]{2,1,0:T(8,128)(2,1)}, u32[]{:S(2)}, u32[]{:S(2)}) collective-permute-start(bf16[4,128,1536]{2,1,0:T(8,128)(2,1)} %pad_maximum_fusion.9), channel_id=1, source_target_pairs={{0,8},{1,9},{2,10},{3,11},{4,12},{5,13},{6,14},{7,15},{8,0},{9,1},... | collective-permute-start | bytes 4718600 | tf_op jit(solution)/shard_map/ppermute | solution.py:797
  182.0 415.6 %reduce-scatter.2.cloned.1.call-start = ((), (), s32[]{:S(2)}) async-start(), calls=%async_computation.7 | async-start | bytes 5898240 | tf_op jit(solution)/shard_map/reduce_scatter | solution.py:1100
  319.6 29.3 %collective-permute-start.26 = (bf16[128,1536]{1,0:T(8,128)(2,1)}, bf16[128,1536]{1,0:T(8,128)(2,1)}, u32[]{:S(2)}, u32[]{:S(2)}) collective-permute-start(bf16[128,1536]{1,0:T(8,128)(2,1)} %get-tuple-element.179), channel_id=1, source_target_pairs={{0,17},{1,16},{2,19},{3,18},{4,21},{5,20},{6,23},{7,22},{8,25},{9,... | collective-permute-start | bytes 1179656 | tf_op jit(solution)/shard_map/ppermute | solution.py:797
  323.3 27.1 %collective-permute-start.25 = (bf16[128,1536]{1,0:T(8,128)(2,1)}, bf16[128,1536]{1,0:T(8,128)(2,1)}, u32[]{:S(2)}, u32[]{:S(2)}) collective-permute-start(bf16[128,1536]{1,0:T(8,128)(2,1)} %get-tuple-element.180), channel_id=1, source_target_pairs={{0,1},{1,0},{2,3},{3,2},{4,5},{5,4},{6,7},{7,6},{8,9},{9,8},{10,11... | collective-permute-start | bytes 1179656 | tf_op jit(solution)/shard_map/ppermute | solution.py:797
  378.1 38.0 %collective-permute-start.38 = (bf16[4,128,1536]{2,1,0:T(8,128)(2,1)}, bf16[4,128,1536]{2,1,0:T(8,128)(2,1)}, u32[]{:S(2)}, u32[]{:S(2)}) collective-permute-start(bf16[4,128,1536]{2,1,0:T(8,128)(2,1)} %pad_maximum_fusion.11), channel_id=1, source_target_pairs={{0,8},{1,9},{2,10},{3,11},{4,12},{5,13},{6,14},{7,15},{8,0},{9,1},... | collective-permute-start | bytes 4718600 | tf_op jit(solution)/shard_map/ppermute | solution.py:797
  475.4 46.2 %collective-permute-start.49 = (bf16[96,1536]{1,0:T(8,128)(2,1)}, bf16[96,1536]{1,0:T(8,128)(2,1)}, u32[]{:S(2)}, u32[]{:S(2)}) collective-permute-start(bf16[96,1536]{1,0:T(8,128)(2,1)} %get-tuple-element.191), channel_id=1, source_target_pairs={{0,2},{2,0},{5,7},{7,5},{8,10},{10,8},{13,15},{15,13},{16,18},{18,... | collective-permute-start | bytes 884744 | tf_op jit(solution)/shard_map/ppermute | solution.py:913
  502.1 53.7 %collective-permute-start.39 = (bf16[4,128,1536]{2,1,0:T(8,128)(2,1)}, bf16[4,128,1536]{2,1,0:T(8,128)(2,1)S(1)}, u32[]{:S(2)}, u32[]{:S(2)}) collective-permute-start(bf16[4,128,1536]{2,1,0:T(8,128)(2,1)} %pad_maximum_fusion.12), channel_id=1, source_target_pairs={{0,8},{1,9},{2,10},{3,11},{4,12},{5,13},{6,14},{7,15},{8,0},{9,1},... | collective-permute-start | bytes 4718600 | tf_op jit(solution)/shard_map/ppermute | solution.py:797
  506.8 47.7 %collective-permute-start.50 = (bf16[96,1536]{1,0:T(8,128)(2,1)}, bf16[96,1536]{1,0:T(8,128)(2,1)}, u32[]{:S(2)}, u32[]{:S(2)}) collective-permute-start(bf16[96,1536]{1,0:T(8,128)(2,1)} %get-tuple-element.193), channel_id=1, source_target_pairs={{1,5},{3,7},{4,0},{6,2},{9,13},{11,15},{12,8},{14,10},{17,21},{19,... | collective-permute-start | bytes 884744 | tf_op jit(solution)/shard_map/ppermute | solution.py:913
  508.1 54.3 %collective-permute-start.43 = (bf16[8,48,512]{2,1,0:T(8,128)(2,1)}, bf16[8,48,512]{2,1,0:T(8,128)(2,1)}, u32[]{:S(2)}, u32[]{:S(2)}) collective-permute-start(bf16[8,48,512]{2,1,0:T(8,128)(2,1)} %get-tuple-element.146), channel_id=1, source_target_pairs={{0,2},{1,3},{2,0},{3,1},{4,6},{5,7},{6,4},{7,5},{8,10},{9,11},{10,... | collective-permute-start | bytes 1179656 | tf_op jit(solution)/shard_map/ppermute | solution.py:797
  521.5 43.6 %collective-permute-start.45 = (bf16[8,48,512]{2,1,0:T(8,128)(2,1)}, bf16[8,48,512]{2,1,0:T(8,128)(2,1)S(1)}, u32[]{:S(2)}, u32[]{:S(2)}) collective-permute-start(bf16[8,48,512]{2,1,0:T(8,128)(2,1)} %get-tuple-element.147), channel_id=1, source_target_pairs={{0,6},{1,7},{2,4},{3,5},{4,2},{5,3},{6,0},{7,1},{8,14},{9,15},{10,... | collective-permute-start | bytes 1179656 | tf_op jit(solution)/shard_map/ppermute | solution.py:797
  525.0 46.2 %collective-permute-start.44 = (bf16[8,48,512]{2,1,0:T(8,128)(2,1)}, bf16[8,48,512]{2,1,0:T(8,128)(2,1)S(1)}, u32[]{:S(2)}, u32[]{:S(2)}) collective-permute-start(bf16[8,48,512]{2,1,0:T(8,128)(2,1)} %get-tuple-element.148), channel_id=1, source_target_pairs={{0,4},{1,5},{2,6},{3,7},{4,0},{5,1},{6,2},{7,3},{8,12},{9,13},{10,... | collective-permute-start | bytes 1179656 | tf_op jit(solution)/shard_map/ppermute | solution.py:797
  597.6 27.6 %all-to-all-start.5 = ((bf16[4,3,384,128]{3,2,1,0:T(8,128)(2,1)}), bf16[4,3,384,128]{3,2,1,0:T(8,128)(2,1)S(1)}, u32[]{:S(2)}, u32[]{:S(2)}) async-start(bf16[4,3,384,128]{3,2,1,0:T(8,128)(2,1)} %bitcast.528), calls=%async_computation.6 | async-start | bytes 2359296 | tf_op jit(solution)/shard_map/all_to_all | solution.py:1106
  (110 other events, 1233.7 us)
Sparse Core Ops, SparseCore 0:
  182.1 90.1 all-gather.2
  414.5 92.1 reduce-scatter.1
